TPU v7x, 32 devices: a whole 2x2x4 slice. The times are simulated.
32 devices in a mesh: row: 8 (over y, x, core), col: 4 (over z).
Axes of the slice: x: 2, y: 2, z: 4, core: 2. Of those that a mesh axis runs over, the one named last changes fastest.
Arguments:
- features_t: float32 [18432, 512], P(('row', 'col')), may hold values from -0.0234375 to 0.0234375
- labels: int32 [512], replicated, may hold values from 0 to 1023
- inv_corr: float32 [18432, 18432], P('row', 'col'), may hold values from -1 to 13, as said below
- heads: float32 [18432, 1024], P('row', 'col'), may hold values from -6 to 6
Outputs:
- inv_corr_new: float32 [18432, 18432], P('row', 'col')
- heads_new: float32 [18432, 1024], P('row', 'col')
Inputs may be any that keep to these rules, and one draw needn't show every extreme that they name: inv_corr is symmetric and positive definite, with smallest eigenvalue above 0.5.
All inputs are finite; a program needn't handle non-finite values.
Results may differ from a plain program's by a relative error of at most 0.0001.
Values sent between devices are 32-bit elements; how exact they have to be, the bound alone decides.
No kernel may reach another device: no remote copies, remote signals or barrier semaphores. Data moves between devices by JAX's collectives and lax.ppermute only.
A program may use at most 192 MiB of HBM per device.

v0:
```python
import jax
import jax.numpy as jnp
from jax import lax
from jax.sharding import PartitionSpec as P

EXAMPLES = 256


def from_root(value, axis, root):
    mine = lax.axis_index(axis) == root
    return lax.psum(jnp.where(mine, value, jnp.zeros_like(value)), axis)


def matmul(left, right):
    return jnp.dot(left, right, precision=lax.Precision.HIGHEST, preferred_element_type=jnp.float32)


def contract_rows(left, right):
    return lax.dot_general(
        left,
        right,
        (((0,), (0,)), ((), ())),
        precision=lax.Precision.HIGHEST,
        preferred_element_type=jnp.float32,
    )


def contract_cols(left, right):
    return lax.dot_general(
        left,
        right,
        (((1,), (1,)), ((), ())),
        precision=lax.Precision.HIGHEST,
        preferred_element_type=jnp.float32,
    )


def invert_system(gram):
    identity_mat = jnp.eye(gram.shape[0], dtype=jnp.float32)
    factor = jnp.linalg.cholesky(identity_mat + gram)
    return jax.scipy.linalg.cho_solve((factor, True), identity_mat)


def gather_columns(panel):
    ratio = lax.axis_size("row") // lax.axis_size("col")
    first = ratio * lax.axis_index("col")
    pieces = [from_root(panel, "row", first + member) for member in range(ratio)]
    return jnp.concatenate(pieces, 0)


def row_panel(tile, columns):
    return lax.psum(matmul(tile, columns), "col")


def fitted_terms(rows_part, panel, head):
    return lax.psum((contract_rows(rows_part, panel), contract_rows(rows_part, head)), "row")


def on_device(features_t, labels, inv_corr, heads):
    rows_all = lax.all_gather(features_t, "col", axis=0, tiled=True)
    cols_all = gather_columns(rows_all)
    width = heads.shape[1]
    classes = lax.axis_index("col") * width + jnp.arange(width, dtype=jnp.int32)
    targets = (labels[:, None] == classes[None, :]).astype(jnp.float32)
    tile = inv_corr
    head = heads
    panel = row_panel(tile, cols_all)
    gram, fitted = fitted_terms(rows_all, panel, head)
    first_rows = panel[:, :EXAMPLES]
    second_rows = panel[:, EXAMPLES:]
    cross_gram = gram[EXAMPLES:, :EXAMPLES]
    inverse_one = invert_system(gram[:EXAMPLES, :EXAMPLES])
    gain_one = matmul(first_rows, inverse_one)
    linked = matmul(cross_gram, inverse_one)
    panel_two = second_rows - contract_cols(gain_one, cross_gram)
    gram_two = gram[EXAMPLES:, EXAMPLES:] - contract_cols(linked, cross_gram)
    resid_one = targets[:EXAMPLES] - fitted[:EXAMPLES]
    resid_two = targets[EXAMPLES:] - fitted[EXAMPLES:] - matmul(linked, resid_one)
    inverse_two = invert_system(gram_two)
    gain_two = matmul(panel_two, inverse_two)
    head = head + matmul(gain_one, resid_one) + matmul(gain_two, resid_two)
    gains = jnp.concatenate([gain_one, gain_two], 1)
    both_cols = gather_columns(jnp.concatenate([first_rows, panel_two], 1))
    tile = tile - contract_cols(gains, both_cols)
    return (tile, head)


def solution(mesh):
    placed = (P(("row", "col"), None), P(), P("row", "col"), P("row", "col"))
    return jax.shard_map(
        on_device,
        mesh=mesh,
        in_specs=placed,
        out_specs=(P("row", "col"), P("row", "col")),
        check_vma=False,
    )
```

profile of v0, /device:TPU:0, one launch (start us, length us, event | category | flops | bytes accessed | tf_op | source)
XLA Modules:
  0.0 886.3 jit_solution(8820467815669776445)
XLA Ops:
  7.2 0.7 all-gather.2.cloned.1.call-update
  8.0 93.7 %all-gather.2.cloned.1.call-done = f32[2304,512]{1,0:T(8,128)} async-done(((f32[576,512]{1,0:T(8,128)}), f32[2304,512]{1,0:T(8,128)}) %all-gather.2.cloned.1.call-update) | async-done | bytes 4718608 | tf_op jit(solution)/shard_map/all_gather | solution.py:60
  101.7 6.0 copy.10
  107.7 6.6 broadcast_select_fusion.1
  114.4 136.2 %all-reduce.14.cloned.1.call-done = (f32[2304,512]{0,1:T(8,128)}, f32[2304,512]{0,1:T(8,128)}) async-done(((f32[2304,512]{0,1:T(8,128)}, f32[2304,512]{0,1:T(8,128)}), (f32[2304,512]{0,1:T(8,128)}, f32[2304,512]{0,1:T(8,128)})) %all-reduce.14.cloned.1.call-update) | async-done | bytes 9437200 | tf_op jit(solution)/shard_map/psum | solution.py:11
  250.6 74.0 %fusion.7 = f32[2304,512]{0,1:T(8,128)} fusion(f32[2304,4608]{1,0:T(8,128)} %param.9, f32[2304,512]{0,1:T(8,128)} %get-tuple-element.39, f32[2304,512]{0,1:T(8,128)} %get-tuple-element.40), kind=kOutput, calls=%fused_computation.12 | convolution fusion | flops 65232175104 | bytes 56623104 | tf_op jit(solution)/shard_map/dot_general | solution.py:15
  324.9 171.9 %all-reduce.8.cloned.1.call-done = f32[2304,512]{0,1:T(8,128)} async-done(((f32[2304,512]{0,1:T(8,128)}), f32[2304,512]{0,1:T(8,128)}) %all-reduce.8.cloned.1.call-update) | async-done | bytes 4718608 | tf_op jit(solution)/shard_map/psum | solution.py:52
  496.8 11.6 %convolution_bitcast_fusion = f32[512,512]{0,1:T(8,128)} fusion(f32[2304,512]{0,1:T(8,128)} %all-reduce.8.cloned.1.call-done, f32[2304,512]{1,0:T(8,128)} %all-gather.2.cloned.1.call-done), kind=kOutput, calls=%fused_computation.24 | convolution fusion | flops 7247757312 | bytes 10485760 | tf_op jit(solution)/shard_map/dot_general | solution.py:19
  508.4 10.6 %fusion.56 = f32[512,256]{1,0:T(8,128)} fusion(f32[2304,512]{1,0:T(8,128)} %all-gather.2.cloned.1.call-done, f32[2304,256]{1,0:T(8,128)S(1)} %copy-done.1), kind=kOutput, calls=%fused_computation.107 | convolution fusion | flops 3623878656 | bytes 7602176 | tf_op jit(solution)/shard_map/dot_general | solution.py:19
  519.0 45.1 %all-reduce.10.cloned.1.call-done = f32[512,512]{0,1:T(8,128)} async-done(((f32[512,512]{0,1:T(8,128)}), f32[512,512]{0,1:T(8,128)}) %all-reduce.10.cloned.1.call-update) | async-done | bytes 1048592 | tf_op jit(solution)/shard_map/psum | solution.py:56
  564.2 1.0 slice_add_fusion
  565.3 1.0 fusion.21
  566.3 11.7 %cholesky.130 = f32[128,128]{1,0:T(8,128)S(1)} custom-call(f32[128,128]{1,0:T(8,128)S(1)} %cholesky.194), custom_call_target="Cholesky" | custom-call | tf_op jit(solution)/shard_map/jit(cholesky)/cholesky | solution.py:40
  578.1 10.2 %custom-call.15 = f32[1,128,128]{1,2,0:T(8,128)S(1)} custom-call(f32[1,128,128]{2,1,0:T(8,128)S(1)} %get-tuple-element.56), custom_call_target="InvertDiagBlocksLowerTriangular" | custom-call | tf_op jit(solution)/shard_map/jit(cholesky)/cholesky | solution.py:40
  588.7 11.7 %cholesky.147 = f32[128,128]{1,0:T(8,128)S(1)} custom-call(f32[128,128]{1,0:T(8,128)S(1)} %convolution_subtract_fusion.9), custom_call_target="Cholesky" | custom-call | tf_op jit(solution)/shard_map/jit(cholesky)/cholesky | solution.py:40
  600.5 0.6 compare_reduce_fusion.2
  602.6 4.0 while.4
  602.6 0.6 fusion.94
  603.2 1.4 bitcast_dynamic-update-slice_fusion.4
  604.6 0.6 fusion.94
  605.2 1.4 bitcast_dynamic-update-slice_fusion.4
  606.6 19.9 %custom-call.16 = f32[2,128,128]{1,2,0:T(8,128)S(1)} custom-call(f32[2,128,128]{2,1,0:T(8,128)S(1)} %get-tuple-element.18), custom_call_target="InvertDiagBlocksLowerTriangular" | custom-call | tf_op jit(solution)/shard_map/jit(_cho_solve)/triangular_solve | solution.py:41
  628.3 3.9 fusion.27
  632.2 4.2 convolution_subtract_fusion.1
  636.5 4.6 fusion.14
  641.1 0.6 copy-done.5
  641.8 0.9 compare_convert_fusion
  642.7 1.5 fusion.24
  644.2 1.6 fusion.15
  646.1 0.7 copy-done.3
  646.8 11.7 %cholesky.164 = f32[128,128]{1,0:T(8,128)S(1)} custom-call(f32[128,128]{1,0:T(8,128)S(1)} %cholesky.197), custom_call_target="Cholesky" | custom-call | tf_op jit(solution)/shard_map/jit(cholesky)/cholesky | solution.py:40
  658.5 10.2 %custom-call.17 = f32[1,128,128]{1,2,0:T(8,128)S(1)} custom-call(f32[1,128,128]{2,1,0:T(8,128)S(1)} %get-tuple-element.52), custom_call_target="InvertDiagBlocksLowerTriangular" | custom-call | tf_op jit(solution)/shard_map/jit(cholesky)/cholesky | solution.py:40
  668.7 1.0 constant_dynamic-update-slice_fusion.1
  669.8 1.1 convolution_subtract_fusion.8
  670.9 11.7 %cholesky.181 = f32[128,128]{1,0:T(8,128)S(1)} custom-call(f32[128,128]{1,0:T(8,128)S(1)} %convolution_subtract_fusion.8), custom_call_target="Cholesky" | custom-call | tf_op jit(solution)/shard_map/jit(cholesky)/cholesky | solution.py:40
  682.6 0.6 compare_reduce_fusion.1
  683.3 0.7 compare_reduce_fusion
  685.2 3.8 while.5
  685.3 0.6 fusion.95
  685.8 1.3 bitcast_dynamic-update-slice_fusion.5
  687.1 0.6 fusion.95
  687.7 1.3 bitcast_dynamic-update-slice_fusion.5
  689.0 19.7 %custom-call.18 = f32[2,128,128]{1,2,0:T(8,128)S(1)} custom-call(f32[2,128,128]{2,1,0:T(8,128)S(1)} %get-tuple-element.19), custom_call_target="InvertDiagBlocksLowerTriangular" | custom-call | tf_op jit(solution)/shard_map/jit(_cho_solve)/triangular_solve | solution.py:41
  710.6 5.4 fusion.16
  716.0 68.0 %all-reduce.12.cloned.1.call-done = (f32[2304,512]{0,1:T(8,128)}, f32[2304,512]{0,1:T(8,128)}, f32[512,256]{1,0:T(8,128)}) async-done(((f32[2304,512]{0,1:T(8,128)}, f32[2304,512]{0,1:T(8,128)}, f32[512,256]{1,0:T(8,128)}), (f32[2304,512]{0,1:T(8,128)}, f32[2304,512]{0,1:T(8,128)}, f32[512,256]{1,0:T(8,128)})) %all-reduce.12.cloned.1.call-update) | async-done | bytes 9961488 | tf_op jit(solution)/shard_map/psum | solution.py:11
  784.0 7.1 convolution_add_fusion.1
  791.6 80.3 %convolution_subtract_fusion = f32[2304,4608]{1,0:T(8,128)} fusion(f32[2304,4608]{1,0:T(8,128)} %param.9, f32[2304,512]{0,1:T(8,128)} %get-tuple-element.36, f32[2304,512]{0,1:T(8,128)} %get-tuple-element.37, f32[2304,256]{0,1:T(8,128)} %fusion.16, f32[2304,256]{0,1:T(8,128)S(1)} %fusion.27), kind=kOutput, calls=%fused_computation.4 | convolution fusion | flops 65243971584 | bytes 99090432 | tf_op jit(solution)/shard_map/dot_general | solution.py:29
  871.9 7.6 convolution_add_fusion
  (59 shorter events, 5.8 us)
Async XLA Ops:
  7.2 94.5 %all-gather.2.cloned.1.call-start = ((), (), s32[]{:S(2)}) async-start(), calls=%async_computation | async-start | bytes 5898240 | tf_op jit(solution)/shard_map/all_gather | solution.py:60
  7.9 242.7 %all-reduce.14.cloned.1.call-start = ((), (), s32[]{:S(2)}) async-start(), calls=%async_computation.4 | async-start | bytes 18874368 | tf_op jit(solution)/shard_map/psum | solution.py:11
  114.4 382.4 %all-reduce.8.cloned.1.call-start = ((), (), s32[]{:S(2)}) async-start(), calls=%async_computation.1 | async-start | bytes 9437184 | tf_op jit(solution)/shard_map/psum | solution.py:52
  324.6 239.6 %all-reduce.10.cloned.1.call-start = ((), (), s32[]{:S(2)}) async-start(), calls=%async_computation.2 | async-start | bytes 2097152 | tf_op jit(solution)/shard_map/psum | solution.py:56
  324.9 183.6 %copy-start.1 = (f32[2304,256]{1,0:T(8,128)S(1)}, f32[2304,256]{1,0:T(8,128)}, u32[]{:S(2)}) copy-start(f32[2304,256]{1,0:T(8,128)} %param.10) | copy-start | bytes 7077892
  508.4 275.6 %all-reduce.12.cloned.1.call-start = ((), (), s32[]{:S(2)}) async-start(), calls=%async_computation.3 | async-start | bytes 19922944 | tf_op jit(solution)/shard_map/psum | solution.py:11
  632.2 4.3 slice-start
  636.5 4.6 copy-start
  641.1 0.7 copy-start.5
  646.1 0.7 copy-start.3
  716.0 75.2 %copy-start.2 = (f32[512,256]{1,0:T(8,128)S(1)}, f32[512,256]{1,0:T(8,128)}, u32[]{:S(2)}) copy-start(f32[512,256]{1,0:T(8,128)} %compare_convert_fusion) | copy-start | bytes 1572868
  784.0 7.2 copy-start.4
Sparse Core Ops, SparseCore 0:
  9.5 92.0 all-gather.1
  114.5 136.0 all-reduce.13
  324.7 172.0 all-reduce.7
  508.5 55.6 all-reduce.9
  641.2 142.7 all-reduce.11
where the time goes:
time: 896 us; the launch traced here: 886 us
  waiting for transfers between devices  516 us (58%)
  matrix products  215 us (24%)
  other arithmetic  123 us (14%)
  between operations  16.9 us (2%)
  local copies, waits for them, and re-layouts  15.5 us (2%)
    psum x2, waiting for transfers between devices, from_root(): return lax.psum(jnp.where(mine, value, jnp.zeros_like(value)), axis)  204 us
    psum x1, waiting for transfers between devices, row_panel(): return lax.psum(matmul(tile, columns), 'col')  172 us
    dot_general x7, matrix products, matmul(): jnp.dot(left, right, precision=lax.Precision.HIGHEST, preferred_element_t...  100 us
    all_gather x1, waiting for transfers between devices, on_device(): rows_all = lax.all_gather(features_t, 'col', axis=0, tiled=True)  93.7 us
    dot_general x3, matrix products, contract_cols(): lax.dot_general(left, right, (((1,), (1,)), ((), ())), precision=lax.Prec...  86.2 us
    another operation x13, other arithmetic, invert_system(): factor = jnp.linalg.cholesky(identity_mat + gram)  69.3 us
    psum x1, waiting for transfers between devices, fitted_terms(): lax.psum((contract_rows(rows_part, panel), contract_rows(rows_part, head)...  45.1 us
    another operation x5, other arithmetic, invert_system(): return jax.scipy.linalg.cho_solve((factor, True), identity_mat)  39.6 us
  transfers between devices with their start and end apart: 5, of which 5 were waited for; matrix products, arithmetic and copies ran while one was open for 9% of the time, Pallas kernels for 0%

commit v1 on v0

v1 whole, which is shorter than its diff:
```python
import math

import jax
import jax.numpy as jnp
from jax import lax
from jax.experimental import pallas as pl
from jax.experimental.pallas import tpu as pltpu
from jax.sharding import PartitionSpec as P

BLOCK = 128
LANES = 128
VMEM = 60 * 1024 * 1024
GROUP = 8
BIG = lax.Precision.HIGH
SMALL = lax.Precision.HIGHEST


def product(left, right, dims, precision):
    return lax.dot_general(left, right, (dims, ((), ())), precision=precision, preferred_element_type=jnp.float32)


def matmul(left, right, precision=SMALL):
    return product(left, right, ((1,), (0,)), precision)


def contract_rows(left, right, precision=SMALL):
    return product(left, right, ((0,), (0,)), precision)


def contract_cols(left, right, precision=SMALL):
    return product(left, right, ((1,), (1,)), precision)


def pick(blocks, index):
    return lax.dynamic_index_in_dim(blocks, index, 0, keepdims=False)


def put(blocks, value, index):
    return lax.dynamic_update_index_in_dim(blocks, value, index, 0)


class Places:
    def __init__(self):
        self.rows = lax.axis_size("row")
        self.cols = lax.axis_size("col")
        self.ratio = self.rows // self.cols
        self.row = lax.axis_index("row")
        self.col = lax.axis_index("col")
        self.chip = self.row // self.ratio
        self.core = self.row % self.ratio
        order = []
        for low in range(self.cols // 2):
            order += [low, self.cols - 1 - low]
        self.order = order
        self.where = [order.index(mask) for mask in range(self.cols)]

    def slot_of(self, col):
        return jnp.asarray(self.where, jnp.int32)[col ^ self.chip]


def flip(value, mask, axis, size):
    return lax.ppermute(value, axis, [(i, i ^ mask) for i in range(size)])


def line_step(above, below, step, at):
    above = lax.ppermute(above, "col", [(i, i - 1) for i in range(1, at.cols - step + 1)])
    below = lax.ppermute(below, "col", [(i, i + 1) for i in range(step - 1, at.cols - 1)])
    return above, below


def split_bits(size):
    bits = []
    mask = 1
    while mask < size:
        bits.append(mask)
        mask *= 2
    return bits


def halve(blocks, bits, index, axis, size, scale=1):
    count = len(bits)
    dims = list(reversed(split_bits(blocks.shape[0])))
    value = blocks.reshape((2,) * count + blocks.shape[1:])
    for bit in bits:
        dim = dims.index(bit)
        dims.remove(bit)
        on = (index // bit) % 2
        keep = lax.dynamic_index_in_dim(value, on, dim, keepdims=False)
        away = lax.dynamic_index_in_dim(value, 1 - on, dim, keepdims=False)
        value = keep + flip(away, bit * scale, axis, size)
    return value


def double(own, bits, index, axis, size, scale=1):
    value, dims = own, []
    for bit in reversed(bits):
        other = flip(value, bit * scale, axis, size)
        at_dim = len([d for d in dims if d > bit])
        dims.append(bit)
        on = (index // bit) % 2
        low = jnp.where(on == 0, value, other)
        high = jnp.where(on == 0, other, value)
        value = jnp.stack([low, high], at_dim)
    return value.reshape((2 ** len(bits),) + own.shape)


def plane_scatter(partial, at):
    mine = partial[0]
    for step in range(1, at.ratio):
        mine = mine + flip(partial[step], step, "row", at.rows)
    bits = split_bits(at.cols)
    part = mine.shape[1] // 2
    top = halve(mine[:, :part], bits, at.chip, "row", at.rows, at.ratio)
    low = halve(mine[:, part:], bits[::-1], at.chip, "row", at.rows, at.ratio)
    return jnp.concatenate([top, low], 0)


def plane_gather(own, at):
    bits = split_bits(at.cols)
    part = own.shape[0] // 2
    top = double(own[:part], bits, at.chip, "row", at.rows, at.ratio)
    low = double(own[part:], bits[::-1], at.chip, "row", at.rows, at.ratio)
    mine = jnp.concatenate([top, low], 1)
    return [mine] + [flip(mine, step, "row", at.rows) for step in range(1, at.ratio)]


def to_line(own, at):
    pairs = []
    for row in range(at.rows):
        for col in range(at.cols):
            target = (at.ratio * col + row // at.cols, at.order[row % at.cols] ^ col)
            pairs.append((row * at.cols + col, target[0] * at.cols + target[1]))
    return lax.ppermute(own, ("row", "col"), pairs)


def sum_to_line(value, at):
    return halve(value.reshape(at.rows, -1, value.shape[1]), split_bits(at.rows), at.row, "row", at.rows)


def sum_from_line(piece, at):
    for bit in split_bits(at.cols):
        piece = piece + flip(piece, bit, "col", at.cols)
    return double(piece, split_bits(at.rows), at.row, "row", at.rows).reshape(-1, piece.shape[1])


def sweep_small(work, flipped):
    size = work.shape[0]
    lanes = lax.broadcasted_iota(jnp.int32, (GROUP, size), 1)
    subs = lax.broadcasted_iota(jnp.int32, (GROUP, size), 0)
    all_lanes = lax.broadcasted_iota(jnp.int32, (size, size), 1)

    def body(group, _):
        first = pl.multiple_of(group * GROUP, GROUP)
        rows = work[pl.ds(first, GROUP), :]
        turned = rows.T
        flipped[...] = turned
        corner = flipped[pl.ds(first, GROUP), :]
        b = {}
        for i in range(GROUP):
            for j in range(i, GROUP):
                b[i, j] = jnp.broadcast_to(corner[i : i + 1, j : j + 1], (GROUP, size))
        get = lambda i, j: b[min(i, j), max(i, j)]
        for k in range(GROUP):
            inv = 1.0 / b[k, k]
            scaled = {j: get(k, j) * inv for j in range(GROUP) if j != k}
            for i in range(GROUP):
                for j in range(i, GROUP):
                    if i != k and j != k:
                        b[i, j] = b[i, j] - get(i, k) * scaled[j]
            for j in range(GROUP):
                if j != k:
                    b[min(k, j), max(k, j)] = scaled[j]
            b[k, k] = -inv
        panel = jnp.zeros((GROUP, size), jnp.float32)
        columns = []
        for j in range(GROUP):
            column = get(0, j)
            for i in range(1, GROUP):
                column = jnp.where(subs == i, get(i, j), column)
            columns.append(column)
            panel = panel - column * rows[j : j + 1, :]
        for j in range(GROUP):
            panel = jnp.where(lanes == first + j, columns[j], panel)
        inside = (all_lanes >= first) & (all_lanes < first + GROUP)
        whole = jnp.where(inside, 0.0, work[...])
        for j in range(GROUP):
            whole = whole - turned[:, j : j + 1] * panel[j : j + 1, :]
        work[...] = whole
        work[pl.ds(first, GROUP), :] = panel
        return 0

    lax.fori_loop(0, size // GROUP, body, 0)


def sweep_kernel(which, last, in_ref, out_ref, work, flipped):
    size = work.shape[0]
    here = slice(which * size, (which + 1) * size)
    work[...] = in_ref[here, here]
    sweep_small(work, flipped)
    corner = work[...]
    dot = lambda x, y: jnp.dot(x, y, precision=lax.Precision.HIGHEST, preferred_element_type=jnp.float32)
    panel = -dot(corner, in_ref[here, :])
    lanes = lax.broadcasted_iota(jnp.int32, panel.shape, 1)
    inside = (lanes >= which * size) & (lanes < (which + 1) * size)
    wide = jnp.concatenate([corner] * (panel.shape[1] // size), 1)
    panel = jnp.where(inside, wide, panel)
    sign = -1.0 if last else 1.0
    for block in range(in_ref.shape[0] // size):
        there = slice(block * size, (block + 1) * size)
        if block == which:
            out_ref[there, :] = panel * sign
        else:
            rows = in_ref[there, :]
            out_ref[there, :] = (jnp.where(inside, 0.0, rows) - dot(rows[:, here], panel)) * sign


def invert(matrix):
    order = matrix.shape[0]
    count = order // BLOCK
    for which in range(count):
        matrix = pl.pallas_call(
            lambda *refs, which=which: sweep_kernel(which, which == count - 1, *refs),
            out_shape=jax.ShapeDtypeStruct((order, order), jnp.float32),
            in_specs=[pl.BlockSpec(memory_space=pltpu.VMEM)],
            out_specs=pl.BlockSpec(memory_space=pltpu.VMEM),
            scratch_shapes=[pltpu.VMEM((BLOCK, BLOCK), jnp.float32), pltpu.VMEM((BLOCK, GROUP), jnp.float32)],
            compiler_params=pltpu.CompilerParams(vmem_limit_bytes=16 * 1024 * 1024),
            cost_estimate=pl.CostEstimate(flops=10_000_000_000, bytes_accessed=2 * 4 * order * order, transcendentals=0),
            name=f"sweep_{which}",
        )(matrix)
    return matrix


def split(value):
    high = value.astype(jnp.bfloat16)
    return high, (value - high.astype(jnp.float32)).astype(jnp.bfloat16)


def three_products(left, right, dims):
    dot = lambda x, y: lax.dot_general(x, y, (dims, ((), ())), preferred_element_type=jnp.float32)
    return dot(left[0], right[1]) + dot(left[1], right[0]) + dot(left[0], right[0])


def product_kernel(more, last, where_ref, block_ref, tile_ref, *refs):
    out_refs, (high_ref, low_ref) = refs[more:-2], refs[-2:]

    @pl.when(pl.program_id(0) == 0)
    def _():
        high_ref[...], low_ref[...] = split(block_ref[...].T)

    value = three_products((high_ref[...], low_ref[...]), split(tile_ref[...]), ((1,), (0,)))
    if more:
        value = value + refs[0][...]
    if not last:
        out_refs[0][...] = value
        return
    turned = value.T
    cores = len(out_refs)
    chips, height = out_refs[0].shape[:2]
    for chip in range(chips):
        rows = [turned[(chip * cores + core) * height : (chip * cores + core + 1) * height] for core in range(cores)]
        for away in range(cores):
            out_refs[away][chip] = choose(rows, where_ref[1] ^ away)


def choose(values, index):
    value = values[0]
    for number in range(1, len(values)):
        value = jnp.where(index == number, values[number], value)
    return value


def product_step(block, tile, before, place, at, last):
    height, examples = block.shape
    chips = LANES // math.gcd(at.ratio * height, LANES)
    width = at.ratio * height * chips
    more = before is not None
    wide = pl.BlockSpec((examples, width), lambda i, s: (0, i))
    if last:
        out_spec = [pl.BlockSpec((chips, height, examples), lambda i, s: (i, 0, 0))] * at.ratio
        out_shape = [jax.ShapeDtypeStruct((at.cols, height, examples), jnp.float32)] * at.ratio
    else:
        out_spec, out_shape = wide, jax.ShapeDtypeStruct((examples, tile.shape[1]), jnp.float32)
    return pl.pallas_call(
        lambda *refs: product_kernel(more, last, *refs),
        grid_spec=pltpu.PrefetchScalarGridSpec(
            num_scalar_prefetch=1,
            grid=(at.cols // chips,),
            in_specs=[pl.BlockSpec((height, examples), lambda i, s: (0, 0)), pl.BlockSpec((height, width), lambda i, s: (s[0], i))]
            + [wide] * more,
            out_specs=out_spec,
            scratch_shapes=[pltpu.VMEM((examples, height), jnp.bfloat16)] * 2,
        ),
        out_shape=out_shape,
        compiler_params=pltpu.CompilerParams(vmem_limit_bytes=VMEM),
        cost_estimate=pl.CostEstimate(flops=6 * height * examples * tile.shape[1], bytes_accessed=4 * (height + 2 * examples) * tile.shape[1], transcendentals=0),
        name="product_last" if last else "product",
    )(jnp.stack([place, at.core]).astype(jnp.int32), block, tile, *([before] * more))


def update_kernel(parts, where_ref, gain_ref, tile_ref, *refs):
    part_refs, (out_ref, high_ref, low_ref) = refs[:parts], refs[parts:]

    @pl.when(pl.program_id(1) == 0)
    def _():
        chips, height = part_refs[0].shape[:2]
        for chip in range(chips):
            rows = [ref[chip] for ref in part_refs]
            for core in range(parts):
                first = (chip * parts + core) * height
                high_ref[first : first + height], low_ref[first : first + height] = split(choose(rows, where_ref[0] ^ core))

    out_ref[...] = tile_ref[...] - three_products(split(gain_ref[...]), (high_ref[...], low_ref[...]), ((1,), (1,)))


def update(tile, gain, parts, at):
    height, examples = parts[0].shape[1:]
    chips = LANES // math.gcd(at.ratio * height, LANES)
    width = at.ratio * height * chips
    block = pl.BlockSpec((height, width), lambda i, j, s: (j, i))
    return pl.pallas_call(
        lambda *refs: update_kernel(len(parts), *refs),
        grid_spec=pltpu.PrefetchScalarGridSpec(
            num_scalar_prefetch=1,
            grid=(tile.shape[1] // width, tile.shape[0] // height),
            in_specs=[pl.BlockSpec((height, examples), lambda i, j, s: (j, 0)), block]
            + [pl.BlockSpec((chips, height, examples), lambda i, j, s: (i, 0, 0))] * len(parts),
            out_specs=block,
            scratch_shapes=[pltpu.VMEM((width, examples), jnp.bfloat16)] * 2,
        ),
        out_shape=jax.ShapeDtypeStruct(tile.shape, jnp.float32),
        compiler_params=pltpu.CompilerParams(vmem_limit_bytes=VMEM),
        cost_estimate=pl.CostEstimate(flops=6 * examples * tile.size, bytes_accessed=8 * tile.size, transcendentals=0),
        name="update",
    )(at.core.reshape(1).astype(jnp.int32), gain, tile, *parts)


def gather_and_multiply(features_t, inv_corr, at):
    height, examples = features_t.shape
    count, col = at.cols, at.col

    blocks = put(jnp.zeros((count, height, examples), jnp.float32), features_t, col)
    partial = product_step(features_t, inv_corr, None, col, at, False)
    above, below = [None], [None]
    high, low = features_t, features_t
    for step in range(1, count):
        high, low = line_step(high, low, step, at)
        high, low, partial = lax.optimization_barrier((high, low, partial))
        above.append(high)
        below.append(low)
        early = count - step
        if step < early:
            block = jnp.where(col + step < count, high, low)
            place = jnp.where(col + step < count, col + step, col - step)
        elif step == early:
            block, place = high + low, (col + step) % count
        else:
            block = jnp.where(col + early < count, below[early] + high, low)
            place = jnp.where(col + early < count, (col - early) % count, (col + early) % count)
        partial = product_step(block, inv_corr, partial, place, at, step == count - 1)
        blocks = put(blocks, block, place)
    return blocks.reshape(count * height, examples), partial


def on_device(features_t, labels, inv_corr, heads):
    at = Places()
    height, examples = features_t.shape
    features, partial = gather_and_multiply(features_t, inv_corr, at)
    owned = plane_scatter(partial, at)

    moved = to_line(owned, at)
    slot = at.slot_of(at.col)
    gram = sum_to_line(contract_rows(lax.dynamic_slice_in_dim(features, slot * height, height, 0), moved), at)
    above, below = [None], [None]
    held = moved, moved
    fitted = contract_rows(features, heads, BIG)
    waits = [(bit, min(at.cols - 1, number)) for number, bit in enumerate(split_bits(at.rows))]
    for step in range(1, at.cols):
        held = line_step(*held, step, at)
        for bit, window in waits:
            if window == step - 1:
                fitted = fitted + flip(fitted, bit, "row", at.rows)
        if step == 1:
            held, gram, owned, fitted = lax.optimization_barrier((held, gram, owned, fitted))
            gram = sum_from_line(gram, at)
            col_side = plane_gather(owned, at)
        elif step < at.cols - 1:
            held, gram, fitted = lax.optimization_barrier((held, gram, fitted))
        above.append(held[0])
        below.append(held[1])
    for bit, window in waits:
        if window >= at.cols - 1:
            fitted = fitted + flip(fitted, bit, "row", at.rows)
    blocks = put(jnp.zeros((at.cols, height, examples), jnp.float32), moved, slot)
    for step in range(1, at.cols):
        blocks = put(blocks, above[step] + below[at.cols - step], at.slot_of((at.col + step) % at.cols))
    row_side = blocks.reshape(at.cols * height, examples)

    inverse = invert(gram + jnp.eye(examples, dtype=jnp.float32))
    width = heads.shape[1]
    classes = at.col * width + jnp.arange(width, dtype=jnp.int32)
    targets = (labels[:, None] == classes[None, :]).astype(jnp.float32)
    gain = matmul(row_side, inverse, BIG)
    head = heads + matmul(gain, targets - fitted, BIG)
    tile = update(inv_corr, gain, col_side, at)
    return (tile, head)


def solution(mesh):
    placed = (P(("row", "col"), None), P(), P("row", "col"), P("row", "col"))
    return jax.shard_map(
        on_device,
        mesh=mesh,
        in_specs=placed,
        out_specs=(P("row", "col"), P("row", "col")),
        check_vma=False,
    )
```

time: 896 us -> 420 us (0.47)
  waiting for transfers between devices: 516 us -> 102 us
  matrix products: 215 us -> 18.9 us
  Pallas kernels: 0 us -> 155 us
  other arithmetic: 123 us -> 30.2 us
  starting transfers between devices: 0.41 us -> 84.2 us
    psum x4 -> x0, waiting for transfers between devices: 421 us -> none  [the longest x2 204 us: from_root(): return lax.psum(jnp.where(mine, value, jnp.zeros_like(value)), axis)]
    dot_general x12 -> x4, matrix products: 208 us -> 18.9 us  [product(): lax.dot_general(left, right, (dims, ((), ())), precision=precision, prefe...]
    pallas_call x0 -> x9, Pallas kernels: none -> 155 us  [the longest x4 71.7 us: product_step(): pl.pallas_call(lambda *refs: product_kernel(more, last, *refs), grid_spec...]
    another operation x18 -> x16, other arithmetic: 109 us -> 4.11 us  [the longest x4 2.34 us: product_step(): jnp.stack([place, at.core]).astype(jnp.int32)]
    ppermute x0 -> x34, waiting for transfers between devices: none -> 102 us  [the longest x21 84.9 us: flip(): return lax.ppermute(value, axis, [(i, i ^ mask) for i in range(size)])]
    all_gather x1 -> x0, waiting for transfers between devices: 93.7 us -> none  [on_device(): rows_all = lax.all_gather(features_t, 'col', axis=0, tiled=True)]
    ppermute x0 -> x34, starting transfers between devices: none -> 84.2 us  [the longest x21 50.6 us: flip(): return lax.ppermute(value, axis, [(i, i ^ mask) for i in range(size)])]
    add x2 -> x14, other arithmetic: 0.97 us -> 15.7 us  [the longest x7 6.85 us: halve(): value = keep + flip(away, bit * scale, axis, size)]
  transfers between devices with their start and end apart: 5 -> 34, of which waited for: 5 -> 18; matrix products, arithmetic and copies ran while one was open for 9% -> 11% of each run, Pallas kernels for 0% -> 20%
where the time goes in v1:
time: 420 us; the launch traced here: 414 us
  Pallas kernels  155 us (37%)
  waiting for transfers between devices  102 us (24%)
  starting transfers between devices  84.2 us (20%)
  other arithmetic  30.2 us (7%)
  matrix products  18.9 us (4%)
  local copies, waits for them, and re-layouts  13.3 us (3%)
  between operations  9.63 us (2%)
    ppermute x21, waiting for transfers between devices, flip(): return lax.ppermute(value, axis, [(i, i ^ mask) for i in range(size)])  84.9 us
    pallas_call x4, Pallas kernels, product_step(): pl.pallas_call(lambda *refs: product_kernel(more, last, *refs), grid_spec...  71.7 us
    pallas_call x1, Pallas kernels, update(): pl.pallas_call(lambda *refs: update_kernel(len(parts), *refs), grid_spec=...  53.4 us
    ppermute x21, starting transfers between devices, flip(): return lax.ppermute(value, axis, [(i, i ^ mask) for i in range(size)])  50.6 us
    pallas_call x4, Pallas kernels, invert(): pl.pallas_call(lambda *refs, which=which: sweep_kernel(which, which == co...  29.9 us
    ppermute x6, starting transfers between devices, line_step(): lax.ppermute(below, 'col', [(i, i + 1) for i in range(step - 1, at.cols -...  24.5 us
    dot_general x4, matrix products, product(): lax.dot_general(left, right, (dims, ((), ())), precision=precision, prefe...  18.9 us
    ppermute x6, waiting for transfers between devices, line_step(): lax.ppermute(above, 'col', [(i, i - 1) for i in range(1, at.cols - step +...  14.9 us
  transfers between devices with their start and end apart: 34, of which 18 were waited for; matrix products, arithmetic and copies ran while one was open for 11% of the time, Pallas kernels for 20%

profile of v1, /device:TPU:0, one launch (start us, length us, event | category | flops | bytes accessed | tf_op | source)
XLA Modules:
  0.0 413.6 jit_solution(794128670722403364)
XLA Ops:
  1.9 5.7 %collective-permute-start.1 = (f32[576,512]{1,0:T(8,128)}, f32[576,512]{1,0:T(8,128)S(1)}, u32[]{:S(2)}, u32[]{:S(2)}) collective-permute-start(f32[576,512]{1,0:T(8,128)} %refs_1_.1), channel_id=1, source_target_pairs={{0,1},{1,2},{2,3},{4,5},{5,6},{6,7},{8,9},{9,10},{10,11},{12,13},{... | collective-permute-start | bytes 3538952 | tf_op jit(solution)/shard_map/ppermute | solution.py:67
  8.8 2.7 broadcast.23.clone
  12.7 17.2 %product.3.refs_3_ = f32[512,4608]{1,0:T(8,128)} custom-call(s32[2]{0:T(128)} %pad_add_fusion.1.refs_0_, f32[576,512]{1,0:T(8,128)} %refs_1_.1, f32[2304,4608]{1,0:T(8,128)} %refs_2_.9), custom_call_target="tpu_custom_call" | custom-call | flops 8153726976 | bytes 29491200 | tf_op jit(solution)/shard_map/product/pallas_call | solution.py:284
  29.9 1.9 collective-permute-done
  34.3 1.7 collective-permute-start.3
  36.6 1.7 bitcast_dynamic-update-slice_fusion.5
  38.2 18.1 %product.4.refs_3_ = f32[512,4608]{1,0:T(8,128)} custom-call(s32[2]{0:T(128)} %pad_add_fusion.2.refs_0_, f32[576,512]{1,0:T(8,128)} %get-tuple-element.47.refs_1_, f32[2304,4608]{1,0:T(8,128)} %refs_2_.9, f32[512,4608]{1,0:T(8,128)} %product.3.refs_3_), custom_call_target="tpu_custom_call" | custom-call | flops 8153726976 | bytes 29491200 | tf_op jit(solution)/shard_map/product/pallas_call | solution.py:284
  56.3 6.1 %collective-permute-done.2 = f32[576,512]{1,0:T(8,128)S(1)} collective-permute-done((f32[576,512]{1,0:T(8,128)S(1)}, f32[576,512]{1,0:T(8,128)S(1)}, u32[]{:S(2)}, u32[]{:S(2)}) %collective-permute-start.2) | collective-permute-done | bytes 1179680 | tf_op jit(solution)/shard_map/ppermute | solution.py:66
  63.7 1.9 collective-permute-start.5
  66.2 3.0 bitcast_dynamic-update-slice_fusion.4
  69.2 18.0 %product.5.refs_3_ = f32[512,4608]{1,0:T(8,128)} custom-call(s32[2]{0:T(128)} %pad_add_fusion.3.refs_0_, f32[576,512]{1,0:T(8,128)} %get-tuple-element.45.refs_1_, f32[2304,4608]{1,0:T(8,128)} %refs_2_.9, f32[512,4608]{1,0:T(8,128)} %product.4.refs_3_), custom_call_target="tpu_custom_call" | custom-call | flops 8153726976 | bytes 29491200 | tf_op jit(solution)/shard_map/product/pallas_call | solution.py:284
  87.2 3.4 collective-permute-done.4
  90.7 1.8 bitcast_dynamic-update-slice_fusion.3
  92.5 18.5 %product_last.1 = (f32[4,576,512]{2,1,0:T(8,128)}, f32[4,576,512]{2,1,0:T(8,128)}) custom-call(s32[2]{0:T(128)} %pad_add_fusion.refs_0_, f32[576,512]{1,0:T(8,128)} %get-tuple-element.43.refs_1_, f32[2304,4608]{1,0:T(8,128)} %refs_2_.9, f32[512,4608]{1,0:T(8,128)} %product.5.refs_3_), custom_call_target="tpu_custom_call" | custom-call | flops 8153726976 | bytes 29491200 | tf_op jit(solution)/shard_map/product_last/pallas_call | solution.py:284
  111.0 8.2 %collective-permute-done.6 = f32[4,576,512]{2,1,0:T(8,128)} collective-permute-done((f32[4,576,512]{2,1,0:T(8,128)}, f32[4,576,512]{2,1,0:T(8,128)}, u32[]{:S(2)}, u32[]{:S(2)}) %collective-permute-start.6) | collective-permute-done | bytes 4718624 | tf_op jit(solution)/shard_map/ppermute | solution.py:62
  119.2 4.9 %add.219 = f32[4,576,512]{2,1,0:T(8,128)S(1)} add(f32[4,576,512]{2,1,0:T(8,128)} %get-tuple-element.31, f32[4,576,512]{2,1,0:T(8,128)} %collective-permute-done.6) | non-fusion elementwise | flops 1179648 | bytes 14155776 | tf_op jit(solution)/shard_map/add | solution.py:110
  129.8 24.4 %collective-permute-done.9 = f32[2,288,512]{2,1,0:T(8,128)} collective-permute-done((f32[2,288,512]{2,1,0:T(8,128)S(1)}, f32[2,288,512]{2,1,0:T(8,128)}, u32[]{:S(2)}, u32[]{:S(2)}) %collective-permute-start.9) | collective-permute-done | bytes 1179680 | tf_op jit(solution)/shard_map/ppermute | solution.py:62
  154.2 1.9 bitcast_add_fusion
  158.9 1.6 collective-permute-start.8
  160.5 10.3 %collective-permute-done.10 = f32[288,512]{1,0:T(8,128)S(1)} collective-permute-done((f32[288,512]{1,0:T(8,128)S(1)}, f32[288,512]{1,0:T(8,128)S(1)}, u32[]{:S(2)}, u32[]{:S(2)}) %collective-permute-start.10) | collective-permute-done | bytes 589856 | tf_op jit(solution)/shard_map/ppermute | solution.py:62
  170.8 2.4 collective-permute-done.8
  175.9 4.4 %fusion = f32[512,512]{1,0:T(8,128)S(1)} fusion(f32[576,512]{1,0:T(8,128)S(1)} %collective-permute-done.11, f32[2304,512]{1,0:T(8,128)} %bitcast.21, s32[]{:T(128)S(6)} %select_n.280), kind=kOutput, calls=%fused_computation.21 | convolution fusion | flops 1811939328 | bytes 3407876 | tf_op jit(solution)/shard_map/dot_general | solution.py:19
  182.1 19.4 %collective-permute-start.14 = (f32[2,2,64,512]{3,2,1,0:T(8,128)}, f32[2,2,64,512]{3,2,1,0:T(8,128)}, u32[]{:S(2)}, u32[]{:S(2)}) collective-permute-start(f32[2,2,64,512]{3,2,1,0:T(8,128)} %dynamic-slice_bitcast_fusion.4), channel_id=1, source_target_pairs={{0,4},{4,0},{8,12},{12,8},{16,20},{20,16},{24,28},{28,24},{1,5},{5... | collective-permute-start | bytes 1572872 | tf_op jit(solution)/shard_map/ppermute | solution.py:62
  202.8 13.8 %collective-permute-start.13 = (f32[576,512]{1,0:T(8,128)}, f32[576,512]{1,0:T(8,128)}, u32[]{:S(2)}, u32[]{:S(2)}) collective-permute-start(f32[576,512]{1,0:T(8,128)} %copy-done.4), channel_id=1, source_target_pairs={{0,1},{1,2},{2,3},{4,5},{5,6},{6,7},{8,9},{9,10},{10,11},{12,13},{... | collective-permute-start | bytes 3538952 | tf_op jit(solution)/shard_map/ppermute | solution.py:67
  219.4 3.0 collective-permute-start.15
  222.4 7.0 %fusion.12 = f32[512,256]{1,0:T(8,128)} fusion(f32[2304,512]{1,0:T(8,128)} %bitcast.21, f32[2304,256]{1,0:T(8,128)S(1)} %copy-done.2), kind=kOutput, calls=%fused_computation.67 | convolution fusion | flops 1811939328 | bytes 7602176 | tf_op jit(solution)/shard_map/dot_general | solution.py:19
  231.8 2.7 collective-permute-start.16
  234.6 2.1 add.245
  241.4 2.5 collective-permute-start.20
  243.9 2.9 collective-permute-done.20
  247.5 3.5 collective-permute-start.21
  258.6 4.8 %collective-permute-start.25 = (f32[512,256]{1,0:T(8,128)}, f32[512,256]{1,0:T(8,128)S(1)}, u32[]{:S(2)}, u32[]{:S(2)}) collective-permute-start(f32[512,256]{1,0:T(8,128)} %add.245), channel_id=1, source_target_pairs={{0,8},{4,12},{8,0},{12,4},{16,24},{20,28},{24,16},{28,20},{1,9},{5... | collective-permute-start | bytes 1572872 | tf_op jit(solution)/shard_map/ppermute | solution.py:62
  268.0 2.9 collective-permute-done.22
  274.3 2.0 collective-permute-done.25
  277.2 14.8 %collective-permute-done.23 = f32[2,64,512]{2,1,0:T(8,128)S(1)} collective-permute-done((f32[2,64,512]{2,1,0:T(8,128)S(1)}, f32[2,64,512]{2,1,0:T(8,128)S(1)}, u32[]{:S(2)}, u32[]{:S(2)}) %collective-permute-start.23) | collective-permute-done | bytes 262176 | tf_op jit(solution)/shard_map/ppermute | solution.py:62
  292.6 3.6 collective-permute-start.31
  296.9 2.2 collective-permute-done.18
  301.5 7.5 %sweep_0.1.refs_0_ = f32[512,512]{1,0:T(8,128)S(1)} custom-call(f32[512,512]{1,0:T(8,128)S(1)} %convert_add_fusion.refs_0_), custom_call_target="tpu_custom_call" | custom-call | flops 10000000000 | bytes 2097152 | tf_op jit(solution)/shard_map/sweep_0/pallas_call | solution.py:221
  308.9 13.9 %collective-permute-done.31 = f32[2,288,512]{2,1,0:T(8,128)S(1)} collective-permute-done((f32[2,288,512]{2,1,0:T(8,128)S(1)}, f32[2,288,512]{2,1,0:T(8,128)S(1)}, u32[]{:S(2)}, u32[]{:S(2)}) %collective-permute-start.31) | collective-permute-done | bytes 1179680 | tf_op jit(solution)/shard_map/ppermute | solution.py:62
  322.9 1.6 collective-permute-done.29
  326.3 7.5 %sweep_1.1.refs_0_ = f32[512,512]{1,0:T(8,128)S(1)} custom-call(f32[512,512]{1,0:T(8,128)S(1)} %sweep_0.1.refs_0_), custom_call_target="tpu_custom_call" | custom-call | flops 10000000000 | bytes 2097152 | tf_op jit(solution)/shard_map/sweep_1/pallas_call | solution.py:221
  333.8 7.5 %sweep_2.1.refs_0_ = f32[512,512]{1,0:T(8,128)S(1)} custom-call(f32[512,512]{1,0:T(8,128)S(1)} %sweep_1.1.refs_0_), custom_call_target="tpu_custom_call" | custom-call | flops 10000000000 | bytes 2097152 | tf_op jit(solution)/shard_map/sweep_2/pallas_call | solution.py:221
  341.6 7.5 %sweep_3.1 = f32[512,512]{1,0:T(8,128)S(1)} custom-call(f32[512,512]{1,0:T(8,128)S(1)} %sweep_2.1.refs_0_), custom_call_target="tpu_custom_call" | custom-call | flops 10000000000 | bytes 2097152 | tf_op jit(solution)/shard_map/sweep_3/pallas_call | solution.py:221
  349.1 1.5 bitcast_dynamic-update-slice_fusion.2
  350.9 1.5 bitcast_dynamic-update-slice_fusion
  352.5 3.9 fusion.13.refs_1_
  356.4 3.6 convolution_add_fusion
  360.0 53.4 %update.1 = f32[2304,4608]{1,0:T(8,128)} custom-call(s32[1]{0:T(128)} %bitcast.refs_0_, f32[2304,512]{1,0:T(8,128)} %copy-done, f32[2304,4608]{1,0:T(8,128)} %refs_2_.9, f32[4,576,512]{2,1,0:T(8,128)} %copy-done.6, f32[4,576,512]{2,1,0:T(8,128)} %collective-permute-done.32.refs_4_), custom_call_target="tpu_custom_call" | custom-call | flops 32614907904 | bytes 84934656 | tf_op jit(solution)/shard_map/update/pallas_call | solution.py:321
  (114 shorter events, 47.6 us)
Async XLA Ops:
  0.6 31.1 %collective-permute-start = (f32[576,512]{1,0:T(8,128)}, f32[576,512]{1,0:T(8,128)S(1)}, u32[]{:S(2)}, u32[]{:S(2)}) collective-permute-start(f32[576,512]{1,0:T(8,128)} %refs_1_.1), channel_id=1, source_target_pairs={{1,0},{2,1},{3,2},{5,4},{6,5},{7,6},{9,8},{10,9},{11,10},{13,12},{... | collective-permute-start | bytes 3538952 | tf_op jit(solution)/shard_map/ppermute | solution.py:66
  1.9 31.1 %collective-permute-start.1 = (f32[576,512]{1,0:T(8,128)}, f32[576,512]{1,0:T(8,128)S(1)}, u32[]{:S(2)}, u32[]{:S(2)}) collective-permute-start(f32[576,512]{1,0:T(8,128)} %refs_1_.1), channel_id=1, source_target_pairs={{0,1},{1,2},{2,3},{4,5},{5,6},{6,7},{8,9},{9,10},{10,11},{12,13},{... | collective-permute-start | bytes 3538952 | tf_op jit(solution)/shard_map/ppermute | solution.py:67
  8.8 2.7 copy-start.3
  33.0 29.4 %collective-permute-start.2 = (f32[576,512]{1,0:T(8,128)S(1)}, f32[576,512]{1,0:T(8,128)S(1)}, u32[]{:S(2)}, u32[]{:S(2)}) collective-permute-start(f32[576,512]{1,0:T(8,128)S(1)} %collective-permute-done), channel_id=1, source_target_pairs={{1,0},{2,1},{5,4},{6,5},{9,8},{10,9},{13,12},{14,13},{17,16},{18,1... | collective-permute-start | bytes 3538952 | tf_op jit(solution)/shard_map/ppermute | solution.py:66
  34.3 28.1 %collective-permute-start.3 = (f32[576,512]{1,0:T(8,128)S(1)}, f32[576,512]{1,0:T(8,128)}, u32[]{:S(2)}, u32[]{:S(2)}) collective-permute-start(f32[576,512]{1,0:T(8,128)S(1)} %collective-permute-done.1), channel_id=1, source_target_pairs={{1,2},{2,3},{5,6},{6,7},{9,10},{10,11},{13,14},{14,15},{17,18},{18... | collective-permute-start | bytes 3538952 | tf_op jit(solution)/shard_map/ppermute | solution.py:67
  62.4 28.2 %collective-permute-start.4 = (f32[576,512]{1,0:T(8,128)S(1)}, f32[576,512]{1,0:T(8,128)S(1)}, u32[]{:S(2)}, u32[]{:S(2)}) collective-permute-start(f32[576,512]{1,0:T(8,128)S(1)} %collective-permute-done.2), channel_id=1, source_target_pairs={{1,0},{5,4},{9,8},{13,12},{17,16},{21,20},{25,24},{29,28}} | collective-permute-start | bytes 3538952 | tf_op jit(solution)/shard_map/ppermute | solution.py:66
  63.7 26.9 %collective-permute-start.5 = (f32[576,512]{1,0:T(8,128)}, f32[576,512]{1,0:T(8,128)}, u32[]{:S(2)}, u32[]{:S(2)}) collective-permute-start(f32[576,512]{1,0:T(8,128)} %collective-permute-done.3), channel_id=1, source_target_pairs={{2,3},{6,7},{10,11},{14,15},{18,19},{22,23},{26,27},{30,31}} | collective-permute-start | bytes 3538952 | tf_op jit(solution)/shard_map/ppermute | solution.py:67
  110.9 8.3 %collective-permute-start.6 = (f32[4,576,512]{2,1,0:T(8,128)}, f32[4,576,512]{2,1,0:T(8,128)}, u32[]{:S(2)}, u32[]{:S(2)}) collective-permute-start(f32[4,576,512]{2,1,0:T(8,128)} %get-tuple-element.32), channel_id=1, source_target_pairs={{0,4},{4,0},{8,12},{12,8},{16,20},{20,16},{24,28},{28,24},{1,5},{5... | collective-permute-start | bytes 14155784 | tf_op jit(solution)/shard_map/ppermute | solution.py:62
  124.7 1.4 copy-start.1
  126.1 28.1 %collective-permute-start.9 = (f32[2,288,512]{2,1,0:T(8,128)S(1)}, f32[2,288,512]{2,1,0:T(8,128)}, u32[]{:S(2)}, u32[]{:S(2)}) collective-permute-start(f32[2,288,512]{2,1,0:T(8,128)S(1)} %dynamic-slice_bitcast_fusion), channel_id=1, source_target_pairs={{0,16},{4,20},{8,24},{12,28},{16,0},{20,4},{24,8},{28,12},{1,17},{... | collective-permute-start | bytes 3538952 | tf_op jit(solution)/shard_map/ppermute | solution.py:62
  128.3 29.0 %collective-permute-start.7 = (f32[2,288,512]{2,1,0:T(8,128)}, f32[2,288,512]{2,1,0:T(8,128)}, u32[]{:S(2)}, u32[]{:S(2)}) collective-permute-start(f32[2,288,512]{2,1,0:T(8,128)} %dynamic-slice_bitcast_fusion.1), channel_id=1, source_target_pairs={{0,8},{4,12},{8,0},{12,4},{16,24},{20,28},{24,16},{28,20},{1,9},{5... | collective-permute-start | bytes 3538952 | tf_op jit(solution)/shard_map/ppermute | solution.py:62
  156.1 14.6 %collective-permute-start.10 = (f32[288,512]{1,0:T(8,128)S(1)}, f32[288,512]{1,0:T(8,128)S(1)}, u32[]{:S(2)}, u32[]{:S(2)}) collective-permute-start(f32[288,512]{1,0:T(8,128)S(1)} %dynamic-slice_bitcast_fusion.2), channel_id=1, source_target_pairs={{0,8},{4,12},{8,0},{12,4},{16,24},{20,28},{24,16},{28,20},{1,9},{5... | collective-permute-start | bytes 1769480 | tf_op jit(solution)/shard_map/ppermute | solution.py:62
  158.9 14.3 %collective-permute-start.8 = (f32[288,512]{1,0:T(8,128)S(1)}, f32[288,512]{1,0:T(8,128)S(1)}, u32[]{:S(2)}, u32[]{:S(2)}) collective-permute-start(f32[288,512]{1,0:T(8,128)S(1)} %dynamic-slice_bitcast_fusion.3), channel_id=1, source_target_pairs={{0,16},{4,20},{8,24},{12,28},{16,0},{20,4},{24,8},{28,12},{1,17},{... | collective-permute-start | bytes 1769480 | tf_op jit(solution)/shard_map/ppermute | solution.py:62
  173.3 1.3 copy-start.12
  173.4 2.5 collective-permute-start.11
  175.8 4.4 %copy-start.4 = (f32[576,512]{1,0:T(8,128)}, f32[576,512]{1,0:T(8,128)S(1)}, u32[]{:S(2)}) copy-start(f32[576,512]{1,0:T(8,128)S(1)} %collective-permute-done.11) | copy-start | bytes 3538948
  180.3 1.0 copy-start.7
  181.2 41.2 %copy-start.2 = (f32[2304,256]{1,0:T(8,128)S(1)}, f32[2304,256]{1,0:T(8,128)}, u32[]{:S(2)}) copy-start(f32[2304,256]{1,0:T(8,128)} %param.11) | copy-start | bytes 7077892
  182.1 34.5 %collective-permute-start.14 = (f32[2,2,64,512]{3,2,1,0:T(8,128)}, f32[2,2,64,512]{3,2,1,0:T(8,128)}, u32[]{:S(2)}, u32[]{:S(2)}) collective-permute-start(f32[2,2,64,512]{3,2,1,0:T(8,128)} %dynamic-slice_bitcast_fusion.4), channel_id=1, source_target_pairs={{0,4},{4,0},{8,12},{12,8},{16,20},{20,16},{24,28},{28,24},{1,5},{5... | collective-permute-start | bytes 1572872 | tf_op jit(solution)/shard_map/ppermute | solution.py:62
  201.5 38.7 %collective-permute-start.12 = (f32[576,512]{1,0:T(8,128)}, f32[576,512]{1,0:T(8,128)}, u32[]{:S(2)}, u32[]{:S(2)}) collective-permute-start(f32[576,512]{1,0:T(8,128)} %copy-done.4), channel_id=1, source_target_pairs={{1,0},{2,1},{3,2},{5,4},{6,5},{7,6},{9,8},{10,9},{11,10},{13,12},{... | collective-permute-start | bytes 3538952 | tf_op jit(solution)/shard_map/ppermute | solution.py:66
  202.8 38.6 %collective-permute-start.13 = (f32[576,512]{1,0:T(8,128)}, f32[576,512]{1,0:T(8,128)}, u32[]{:S(2)}, u32[]{:S(2)}) collective-permute-start(f32[576,512]{1,0:T(8,128)} %copy-done.4), channel_id=1, source_target_pairs={{0,1},{1,2},{2,3},{4,5},{5,6},{6,7},{8,9},{9,10},{10,11},{12,13},{... | collective-permute-start | bytes 3538952 | tf_op jit(solution)/shard_map/ppermute | solution.py:67
  217.9 0.8 copy-start.9
  219.4 10.0 %collective-permute-start.15 = (f32[2,64,512]{2,1,0:T(8,128)}, f32[2,64,512]{2,1,0:T(8,128)}, u32[]{:S(2)}, u32[]{:S(2)}) collective-permute-start(f32[2,64,512]{2,1,0:T(8,128)} %dynamic-slice_bitcast_fusion.5), channel_id=1, source_target_pairs={{0,8},{4,12},{8,0},{12,4},{16,24},{20,28},{24,16},{28,20},{1,9},{5... | collective-permute-start | bytes 786440 | tf_op jit(solution)/shard_map/ppermute | solution.py:62
  229.4 5.2 %collective-permute-start.17 = (f32[512,256]{1,0:T(8,128)}, f32[512,256]{1,0:T(8,128)}, u32[]{:S(2)}, u32[]{:S(2)}) collective-permute-start(f32[512,256]{1,0:T(8,128)} %fusion.12), channel_id=1, source_target_pairs={{0,4},{4,0},{8,12},{12,8},{16,20},{20,16},{24,28},{28,24},{1,5},{5... | collective-permute-start | bytes 1572872 | tf_op jit(solution)/shard_map/ppermute | solution.py:62
  230.5 0.7 copy-start.10
  231.8 6.2 %collective-permute-start.16 = (f32[64,512]{1,0:T(8,128)}, f32[64,512]{1,0:T(8,128)}, u32[]{:S(2)}, u32[]{:S(2)}) collective-permute-start(f32[64,512]{1,0:T(8,128)} %dynamic-slice_bitcast_fusion.6), channel_id=1, source_target_pairs={{0,16},{4,20},{8,24},{12,28},{16,0},{20,4},{24,8},{28,12},{1,17},{... | collective-permute-start | bytes 393224 | tf_op jit(solution)/shard_map/ppermute | solution.py:62
  234.6 3.5 copy-start.11
  241.4 5.4 %collective-permute-start.20 = (f32[64,512]{1,0:T(8,128)S(1)}, f32[64,512]{1,0:T(8,128)S(1)}, u32[]{:S(2)}, u32[]{:S(2)}) collective-permute-start(f32[64,512]{1,0:T(8,128)S(1)} %bitcast_add_fusion.6), channel_id=1, source_target_pairs={{0,1},{1,0},{2,3},{3,2},{4,5},{5,4},{6,7},{7,6},{8,9},{9,8},{10,11... | collective-permute-start | bytes 393224 | tf_op jit(solution)/shard_map/ppermute | solution.py:62
  247.5 15.9 %collective-permute-start.21 = (f32[64,512]{1,0:T(8,128)}, f32[64,512]{1,0:T(8,128)}, u32[]{:S(2)}, u32[]{:S(2)}) collective-permute-start(f32[64,512]{1,0:T(8,128)} %add.246), channel_id=1, source_target_pairs={{0,2},{1,3},{2,0},{3,1},{4,6},{5,7},{6,4},{7,5},{8,10},{9,11},{10,... | collective-permute-start | bytes 393224 | tf_op jit(solution)/shard_map/ppermute | solution.py:62
  258.6 17.8 %collective-permute-start.25 = (f32[512,256]{1,0:T(8,128)}, f32[512,256]{1,0:T(8,128)S(1)}, u32[]{:S(2)}, u32[]{:S(2)}) collective-permute-start(f32[512,256]{1,0:T(8,128)} %add.245), channel_id=1, source_target_pairs={{0,8},{4,12},{8,0},{12,4},{16,24},{20,28},{24,16},{28,20},{1,9},{5... | collective-permute-start | bytes 1572872 | tf_op jit(solution)/shard_map/ppermute | solution.py:62
  264.4 6.4 %collective-permute-start.22 = (f32[64,512]{1,0:T(8,128)S(1)}, f32[64,512]{1,0:T(8,128)S(1)}, u32[]{:S(2)}, u32[]{:S(2)}) collective-permute-start(f32[64,512]{1,0:T(8,128)S(1)} %add.247), channel_id=1, source_target_pairs={{0,16},{4,20},{8,24},{12,28},{16,0},{20,4},{24,8},{28,12},{1,17},{... | collective-permute-start | bytes 393224 | tf_op jit(solution)/shard_map/ppermute | solution.py:62
  265.8 26.4 %collective-permute-start.28 = (f32[288,512]{1,0:T(8,128)S(1)}, f32[288,512]{1,0:T(8,128)S(1)}, u32[]{:S(2)}, u32[]{:S(2)}) collective-permute-start(f32[288,512]{1,0:T(8,128)S(1)} %get-tuple-element.60), channel_id=1, source_target_pairs={{0,16},{4,20},{8,24},{12,28},{16,0},{20,4},{24,8},{28,12},{1,17},{... | collective-permute-start | bytes 1769480 | tf_op jit(solution)/shard_map/ppermute | solution.py:62
  266.6 25.6 %collective-permute-start.30 = (f32[288,512]{1,0:T(8,128)S(1)}, f32[288,512]{1,0:T(8,128)S(1)}, u32[]{:S(2)}, u32[]{:S(2)}) collective-permute-start(f32[288,512]{1,0:T(8,128)S(1)} %get-tuple-element.61), channel_id=1, source_target_pairs={{0,8},{4,12},{8,0},{12,4},{16,24},{20,28},{24,16},{28,20},{1,9},{5... | collective-permute-start | bytes 1769480 | tf_op jit(solution)/shard_map/ppermute | solution.py:62
  270.9 1.9 copy-start.5
  270.9 21.2 %collective-permute-start.23 = (f32[2,64,512]{2,1,0:T(8,128)S(1)}, f32[2,64,512]{2,1,0:T(8,128)S(1)}, u32[]{:S(2)}, u32[]{:S(2)}) collective-permute-start(f32[2,64,512]{2,1,0:T(8,128)S(1)} %pad_maximum_fusion.8), channel_id=1, source_target_pairs={{0,8},{4,12},{8,0},{12,4},{16,24},{20,28},{24,16},{28,20},{1,9},{5... | collective-permute-start | bytes 786440 | tf_op jit(solution)/shard_map/ppermute | solution.py:62
  272.8 4.3 %copy-start.8 = (f32[512,256]{1,0:T(8,128)S(1)}, f32[512,256]{1,0:T(8,128)}, u32[]{:S(2)}) copy-start(f32[512,256]{1,0:T(8,128)} %add.245) | copy-start | bytes 1572868
  272.9 26.2 %collective-permute-start.18 = (f32[576,512]{1,0:T(8,128)}, f32[576,512]{1,0:T(8,128)S(1)}, u32[]{:S(2)}, u32[]{:S(2)}) collective-permute-start(f32[576,512]{1,0:T(8,128)} %collective-permute-done.12), channel_id=1, source_target_pairs={{1,0},{2,1},{5,4},{6,5},{9,8},{10,9},{13,12},{14,13},{17,16},{18,1... | collective-permute-start | bytes 3538952 | tf_op jit(solution)/shard_map/ppermute | solution.py:66
  276.4 22.8 %collective-permute-start.19 = (f32[576,512]{1,0:T(8,128)}, f32[576,512]{1,0:T(8,128)S(1)}, u32[]{:S(2)}, u32[]{:S(2)}) collective-permute-start(f32[576,512]{1,0:T(8,128)} %collective-permute-done.13), channel_id=1, source_target_pairs={{1,2},{2,3},{5,6},{6,7},{9,10},{10,11},{13,14},{14,15},{17,18},{18... | collective-permute-start | bytes 3538952 | tf_op jit(solution)/shard_map/ppermute | solution.py:67
  292.1 4.6 %collective-permute-start.24 = (f32[2,2,64,512]{3,2,1,0:T(8,128)S(1)}, f32[2,2,64,512]{3,2,1,0:T(8,128)S(1)}, u32[]{:S(2)}, u32[]{:S(2)}) collective-permute-start(f32[2,2,64,512]{3,2,1,0:T(8,128)S(1)} %pad_maximum_fusion.7), channel_id=1, source_target_pairs={{0,4},{4,0},{8,12},{12,8},{16,20},{20,16},{24,28},{28,24},{1,5},{5... | collective-permute-start | bytes 1572872 | tf_op jit(solution)/shard_map/ppermute | solution.py:62
  292.6 30.2 %collective-permute-start.31 = (f32[2,288,512]{2,1,0:T(8,128)S(1)}, f32[2,288,512]{2,1,0:T(8,128)S(1)}, u32[]{:S(2)}, u32[]{:S(2)}) collective-permute-start(f32[2,288,512]{2,1,0:T(8,128)S(1)} %pad_maximum_fusion.5), channel_id=1, source_target_pairs={{0,16},{4,20},{8,24},{12,28},{16,0},{20,4},{24,8},{28,12},{1,17},{... | collective-permute-start | bytes 3538952 | tf_op jit(solution)/shard_map/ppermute | solution.py:62
  296.4 28.1 %collective-permute-start.29 = (f32[2,288,512]{2,1,0:T(8,128)S(1)}, f32[2,288,512]{2,1,0:T(8,128)S(1)}, u32[]{:S(2)}, u32[]{:S(2)}) collective-permute-start(f32[2,288,512]{2,1,0:T(8,128)S(1)} %pad_maximum_fusion.4), channel_id=1, source_target_pairs={{0,8},{4,12},{8,0},{12,4},{16,24},{20,28},{24,16},{28,20},{1,9},{5... | collective-permute-start | bytes 3538952 | tf_op jit(solution)/shard_map/ppermute | solution.py:62
  299.1 50.0 %collective-permute-start.26 = (f32[576,512]{1,0:T(8,128)S(1)}, f32[576,512]{1,0:T(8,128)S(1)}, u32[]{:S(2)}, u32[]{:S(2)}) collective-permute-start(f32[576,512]{1,0:T(8,128)S(1)} %collective-permute-done.19), channel_id=1, source_target_pairs={{2,3},{6,7},{10,11},{14,15},{18,19},{22,23},{26,27},{30,31}} | collective-permute-start | bytes 3538952 | tf_op jit(solution)/shard_map/ppermute | solution.py:67
  299.9 51.1 %collective-permute-start.27 = (f32[576,512]{1,0:T(8,128)S(1)}, f32[576,512]{1,0:T(8,128)S(1)}, u32[]{:S(2)}, u32[]{:S(2)}) collective-permute-start(f32[576,512]{1,0:T(8,128)S(1)} %collective-permute-done.18), channel_id=1, source_target_pairs={{1,0},{5,4},{9,8},{13,12},{17,16},{21,20},{25,24},{29,28}} | collective-permute-start | bytes 3538952 | tf_op jit(solution)/shard_map/ppermute | solution.py:66
  326.2 7.6 %copy-start.6 = (f32[4,576,512]{2,1,0:T(8,128)}, f32[4,576,512]{2,1,0:T(8,128)S(1)}, u32[]{:S(2)}) copy-start(f32[4,576,512]{2,1,0:T(8,128)S(1)} %pad_maximum_fusion.refs_3_) | copy-start | bytes 14155780
  326.2 33.8 %collective-permute-start.32 = (f32[4,576,512]{2,1,0:T(8,128)S(1)}, f32[4,576,512]{2,1,0:T(8,128)}, u32[]{:S(2)}, u32[]{:S(2)}) collective-permute-start(f32[4,576,512]{2,1,0:T(8,128)S(1)} %pad_maximum_fusion.refs_3_), channel_id=1, source_target_pairs={{0,4},{4,0},{8,12},{12,8},{16,20},{20,16},{24,28},{28,24},{1,5},{5... | collective-permute-start | bytes 14155784 | tf_op jit(solution)/shard_map/ppermute | solution.py:62
  341.3 15.1 %collective-permute-start.33 = (f32[512,256]{1,0:T(8,128)S(1)}, f32[512,256]{1,0:T(8,128)S(1)}, u32[]{:S(2)}, u32[]{:S(2)}) collective-permute-start(f32[512,256]{1,0:T(8,128)S(1)} %add.248), channel_id=1, source_target_pairs={{0,16},{4,20},{8,24},{12,28},{16,0},{20,4},{24,8},{28,12},{1,17},{... | collective-permute-start | bytes 1572872 | tf_op jit(solution)/shard_map/ppermute | solution.py:62
  352.5 3.9 copy-start.13
  356.4 3.6 copy-start

commit v2 on v1

--- a/solution.py
+++ b/solution.py
@@ -1,5 +1,3 @@
-import math
-
 import jax
 import jax.numpy as jnp
 from jax import lax
@@ -8,7 +6,7 @@
 from jax.sharding import PartitionSpec as P
 
 BLOCK = 128
-LANES = 128
+WIDE = 768
 VMEM = 60 * 1024 * 1024
 GROUP = 8
 BIG = lax.Precision.HIGH
@@ -48,14 +46,22 @@
         self.col = lax.axis_index("col")
         self.chip = self.row // self.ratio
         self.core = self.row % self.ratio
-        order = []
-        for low in range(self.cols // 2):
-            order += [low, self.cols - 1 - low]
-        self.order = order
-        self.where = [order.index(mask) for mask in range(self.cols)]
-
-    def slot_of(self, col):
-        return jnp.asarray(self.where, jnp.int32)[col ^ self.chip]
+        self.piece = self.chip ^ choose([jnp.int32(reverse_bits(col, self.cols)) for col in range(self.cols)], self.col)
+
+
+def reverse_bits(value, size):
+    result, mask = 0, 1
+    while mask < size:
+        result = 2 * result + value // mask % 2
+        mask *= 2
+    return result
+
+
+def choose(values, index):
+    value = values[0]
+    for number in range(1, len(values)):
+        value = jnp.where(index == number, values[number], value)
+    return value
 
 
 def flip(value, mask, axis, size):
@@ -104,33 +110,33 @@
     return value.reshape((2 ** len(bits),) + own.shape)
 
 
-def plane_scatter(partial, at):
-    mine = partial[0]
-    for step in range(1, at.ratio):
-        mine = mine + flip(partial[step], step, "row", at.rows)
+def plane_scatter(mine, at):
     bits = split_bits(at.cols)
     part = mine.shape[1] // 2
-    top = halve(mine[:, :part], bits, at.chip, "row", at.rows, at.ratio)
-    low = halve(mine[:, part:], bits[::-1], at.chip, "row", at.rows, at.ratio)
+    top = halve(mine[:, :part], bits, at.piece, "row", at.rows, at.ratio)
+    low = halve(mine[:, part:], bits[::-1], at.piece, "row", at.rows, at.ratio)
     return jnp.concatenate([top, low], 0)
 
 
-def plane_gather(own, at):
-    bits = split_bits(at.cols)
-    part = own.shape[0] // 2
-    top = double(own[:part], bits, at.chip, "row", at.rows, at.ratio)
-    low = double(own[part:], bits[::-1], at.chip, "row", at.rows, at.ratio)
-    mine = jnp.concatenate([top, low], 1)
-    return [mine] + [flip(mine, step, "row", at.rows) for step in range(1, at.ratio)]
-
-
-def to_line(own, at):
-    pairs = []
+def line_pairs(at):
     for row in range(at.rows):
         for col in range(at.cols):
-            target = (at.ratio * col + row // at.cols, at.order[row % at.cols] ^ col)
-            pairs.append((row * at.cols + col, target[0] * at.cols + target[1]))
+            chip, core = row // at.ratio, row % at.ratio
+            yield (row, col), (at.ratio * col + core, chip ^ reverse_bits(col, at.cols))
+
+
+def to_line(own, at):
+    pairs = [(row * at.cols + col, to_row * at.cols + to_col) for (row, col), (to_row, to_col) in line_pairs(at)]
     return lax.ppermute(own, ("row", "col"), pairs)
+
+
+def to_plane(own, at):
+    within, along = [], []
+    for (row, col), (from_row, from_col) in line_pairs(at):
+        within.append((from_row * at.cols + from_col, row * at.cols + from_col))
+        along.append((row * at.cols + from_col, row * at.cols + col))
+    between = lax.ppermute(own, ("row", "col"), within)
+    return lambda hold: lax.ppermute(lax.optimization_barrier((between, hold))[0], ("row", "col"), along)
 
 
 def sum_to_line(value, at):
@@ -242,91 +248,88 @@
 
 
 def product_kernel(more, last, where_ref, block_ref, tile_ref, *refs):
-    out_refs, (high_ref, low_ref) = refs[more:-2], refs[-2:]
+    out_ref, left_ref = refs[-2:]
 
     @pl.when(pl.program_id(0) == 0)
     def _():
-        high_ref[...], low_ref[...] = split(block_ref[...].T)
-
-    value = three_products((high_ref[...], low_ref[...]), split(tile_ref[...]), ((1,), (0,)))
+        high, low = split(block_ref[...].T)
+        left_ref[...] = jnp.concatenate([high, high, low], 1)
+
+    high, low = split(tile_ref[...])
+    right = jnp.concatenate([high, low, high], 0)
+    value = jnp.dot(left_ref[...], right, preferred_element_type=jnp.float32)
     if more:
         value = value + refs[0][...]
-    if not last:
-        out_refs[0][...] = value
-        return
-    turned = value.T
-    cores = len(out_refs)
-    chips, height = out_refs[0].shape[:2]
-    for chip in range(chips):
-        rows = [turned[(chip * cores + core) * height : (chip * cores + core + 1) * height] for core in range(cores)]
-        for away in range(cores):
-            out_refs[away][chip] = choose(rows, where_ref[1] ^ away)
-
-
-def choose(values, index):
-    value = values[0]
-    for number in range(1, len(values)):
-        value = jnp.where(index == number, values[number], value)
-    return value
-
-
-def product_step(block, tile, before, place, at, last):
+    out_ref[...] = value.T if last else value
+
+
+def block_width(half):
+    return max(width for width in range(BLOCK, WIDE + 1, BLOCK) if half % width == 0)
+
+
+def product_step(block, tile, before, place, at, core=None):
     height, examples = block.shape
-    chips = LANES // math.gcd(at.ratio * height, LANES)
-    width = at.ratio * height * chips
-    more = before is not None
-    wide = pl.BlockSpec((examples, width), lambda i, s: (0, i))
+    half = tile.shape[1] // at.ratio
+    width = block_width(half)
+    more, last = before is not None, core is not None
+    steps = (half if last else tile.shape[1]) // width
+    first = core * (half // width) if last else 0
+    wide = pl.BlockSpec((examples, width), lambda i, s: (0, s[1] + i))
     if last:
-        out_spec = [pl.BlockSpec((chips, height, examples), lambda i, s: (i, 0, 0))] * at.ratio
-        out_shape = [jax.ShapeDtypeStruct((at.cols, height, examples), jnp.float32)] * at.ratio
+        out_spec, out_shape = pl.BlockSpec((width, examples), lambda i, s: (i, 0)), (half, examples)
     else:
-        out_spec, out_shape = wide, jax.ShapeDtypeStruct((examples, tile.shape[1]), jnp.float32)
+        out_spec, out_shape = wide, (examples, tile.shape[1])
     return pl.pallas_call(
         lambda *refs: product_kernel(more, last, *refs),
         grid_spec=pltpu.PrefetchScalarGridSpec(
             num_scalar_prefetch=1,
-            grid=(at.cols // chips,),
-            in_specs=[pl.BlockSpec((height, examples), lambda i, s: (0, 0)), pl.BlockSpec((height, width), lambda i, s: (s[0], i))]
+            grid=(steps,),
+            in_specs=[pl.BlockSpec((height, examples), lambda i, s: (0, 0)), pl.BlockSpec((height, width), lambda i, s: (s[0], s[1] + i))]
             + [wide] * more,
             out_specs=out_spec,
-            scratch_shapes=[pltpu.VMEM((examples, height), jnp.bfloat16)] * 2,
+            scratch_shapes=[pltpu.VMEM((examples, 3 * height), jnp.bfloat16)],
         ),
-        out_shape=out_shape,
+        out_shape=jax.ShapeDtypeStruct(out_shape, jnp.float32),
         compiler_params=pltpu.CompilerParams(vmem_limit_bytes=VMEM),
-        cost_estimate=pl.CostEstimate(flops=6 * height * examples * tile.shape[1], bytes_accessed=4 * (height + 2 * examples) * tile.shape[1], transcendentals=0),
+        cost_estimate=pl.CostEstimate(flops=6 * height * examples * steps * width, bytes_accessed=4 * (height + 2 * examples) * steps * width, transcendentals=0),
         name="product_last" if last else "product",
-    )(jnp.stack([place, at.core]).astype(jnp.int32), block, tile, *([before] * more))
-
-
-def update_kernel(parts, where_ref, gain_ref, tile_ref, *refs):
-    part_refs, (out_ref, high_ref, low_ref) = refs[:parts], refs[parts:]
-
-    @pl.when(pl.program_id(1) == 0)
+    )(jnp.stack([jnp.int32(place), jnp.int32(first)]), block, tile, *([before] * more))
+
+
+def update_kernel(parts, steps, where_ref, gain_ref, tile_ref, *refs):
+    part_refs, (out_ref, left_ref, right_ref) = refs[:parts], refs[parts:]
+    step = pl.program_id(0)
+
+    @pl.when(step == 0)
     def _():
-        chips, height = part_refs[0].shape[:2]
-        for chip in range(chips):
-            rows = [ref[chip] for ref in part_refs]
-            for core in range(parts):
-                first = (chip * parts + core) * height
-                high_ref[first : first + height], low_ref[first : first + height] = split(choose(rows, where_ref[0] ^ core))
-
-    out_ref[...] = tile_ref[...] - three_products(split(gain_ref[...]), (high_ref[...], low_ref[...]), ((1,), (1,)))
+        high, low = split(gain_ref[...])
+        left_ref[...] = jnp.concatenate([high, high, low], 1)
+
+    for away in range(parts):
+
+        @pl.when(step // steps == away)
+        def _():
+            high, low = split(part_refs[away][...])
+            right_ref[...] = jnp.concatenate([high, low, high], 1)
+
+    change = lax.dot_general(left_ref[...], right_ref[...], (((1,), (1,)), ((), ())), preferred_element_type=jnp.float32)
+    out_ref[...] = tile_ref[...] - change
 
 
 def update(tile, gain, parts, at):
-    height, examples = parts[0].shape[1:]
-    chips = LANES // math.gcd(at.ratio * height, LANES)
-    width = at.ratio * height * chips
-    block = pl.BlockSpec((height, width), lambda i, j, s: (j, i))
+    half, examples = parts[0].shape
+    width = block_width(half)
+    steps = half // width
+    block = pl.BlockSpec((tile.shape[0], width), lambda i, s: (0, ((i // steps) ^ s[0]) * steps + i % steps))
+    part = lambda away: pl.BlockSpec((width, examples), lambda i, s: (jnp.clip(i - away * steps, 0, steps - 1), 0))
     return pl.pallas_call(
-        lambda *refs: update_kernel(len(parts), *refs),
+        lambda *refs: update_kernel(len(parts), steps, *refs),
         grid_spec=pltpu.PrefetchScalarGridSpec(
             num_scalar_prefetch=1,
-            grid=(tile.shape[1] // width, tile.shape[0] // height),
-            in_specs=[pl.BlockSpec((height, examples), lambda i, j, s: (j, 0)), block]
-            + [pl.BlockSpec((chips, height, examples), lambda i, j, s: (i, 0, 0))] * len(parts),
+            grid=(steps * len(parts),),
+            in_specs=[pl.BlockSpec(gain.shape, lambda i, s: (0, 0)), block] + [part(away) for away in range(len(parts))],
             out_specs=block,
-            scratch_shapes=[pltpu.VMEM((width, examples), jnp.bfloat16)] * 2,
+            scratch_shapes=[pltpu.VMEM((gain.shape[0], 3 * examples), jnp.bfloat16), pltpu.VMEM((width, 3 * examples), jnp.bfloat16)],
         ),
         out_shape=jax.ShapeDtypeStruct(tile.shape, jnp.float32),
         compiler_params=pltpu.CompilerParams(vmem_limit_bytes=VMEM),
@@ -340,7 +343,7 @@
     count, col = at.cols, at.col
 
     blocks = put(jnp.zeros((count, height, examples), jnp.float32), features_t, col)
-    partial = product_step(features_t, inv_corr, None, col, at, False)
+    partial = product_step(features_t, inv_corr, None, col, at)
     above, below = [None], [None]
     high, low = features_t, features_t
     for step in range(1, count):
@@ -357,43 +360,47 @@
         else:
             block = jnp.where(col + early < count, below[early] + high, low)
             place = jnp.where(col + early < count, (col - early) % count, (col + early) % count)
-        partial = product_step(block, inv_corr, partial, place, at, step == count - 1)
         blocks = put(blocks, block, place)
-    return blocks.reshape(count * height, examples), partial
+        if step < count - 1:
+            partial = product_step(block, inv_corr, partial, place, at)
+    mine = None
+    for away in reversed(range(at.ratio)):
+        rows = product_step(block, inv_corr, partial, place, at, at.core ^ away)
+        if away > 0:
+            rows = flip(rows, away, "row", at.rows)
+        mine = rows if mine is None else mine + rows
+    return blocks.reshape(count * height, examples), mine.reshape(count, height, examples)
 
 
 def on_device(features_t, labels, inv_corr, heads):
     at = Places()
     height, examples = features_t.shape
-    features, partial = gather_and_multiply(features_t, inv_corr, at)
-    owned = plane_scatter(partial, at)
-
+    own_rows = to_plane(features_t, at)
+    features, mine = gather_and_multiply(features_t, inv_corr, at)
+    own_rows = own_rows(features)
+    fitted = contract_rows(features, heads, BIG)
+    owned = plane_scatter(mine, at)
+    owned, fitted = lax.optimization_barrier((owned, fitted))
+
+    gram = sum_to_line(contract_rows(own_rows, owned), at)
     moved = to_line(owned, at)
-    slot = at.slot_of(at.col)
-    gram = sum_to_line(contract_rows(lax.dynamic_slice_in_dim(features, slot * height, height, 0), moved), at)
-    above, below = [None], [None]
-    held = moved, moved
-    fitted = contract_rows(features, heads, BIG)
-    waits = [(bit, min(at.cols - 1, number)) for number, bit in enumerate(split_bits(at.rows))]
+    lines = [line_step(moved, moved, 1, at)]
+    gated = lax.optimization_barrier((owned, gram))[0]
+    gram = sum_from_line(gram, at)
+    part = height // 2
+    bits = split_bits(at.cols)
+    top = double(gated[:part], bits, at.piece, "row", at.rows, at.ratio)
+    low = double(gated[part:], bits[::-1], at.piece, "row", at.rows, at.ratio)
+    half = jnp.concatenate([top, low], 1).reshape(at.cols * height, examples)
+    col_side = [half] + [flip(half, away, "row", at.rows) for away in range(1, at.ratio)]
+    for bit in split_bits(at.rows):
+        fitted = fitted + flip(fitted, bit, "row", at.rows)
+
+    for step in range(2, at.cols):
+        lines.append(line_step(*lines[-1], step, at))
+    blocks = put(jnp.zeros((at.cols, height, examples), jnp.float32), moved, at.col)
     for step in range(1, at.cols):
-        held = line_step(*held, step, at)
-        for bit, window in waits:
-            if window == step - 1:
-                fitted = fitted + flip(fitted, bit, "row", at.rows)
-        if step == 1:
-            held, gram, owned, fitted = lax.optimization_barrier((held, gram, owned, fitted))
-            gram = sum_from_line(gram, at)
-            col_side = plane_gather(owned, at)
-        elif step < at.cols - 1:
-            held, gram, fitted = lax.optimization_barrier((held, gram, fitted))
-        above.append(held[0])
-        below.append(held[1])
-    for bit, window in waits:
-        if window >= at.cols - 1:
-            fitted = fitted + flip(fitted, bit, "row", at.rows)
-    blocks = put(jnp.zeros((at.cols, height, examples), jnp.float32), moved, slot)
-    for step in range(1, at.cols):
-        blocks = put(blocks, above[step] + below[at.cols - step], at.slot_of((at.col + step) % at.cols))
+        blocks = put(blocks, lines[step - 1][0] + lines[at.cols - step - 1][1], (at.col + step) % at.cols)
     row_side = blocks.reshape(at.cols * height, examples)
 
     inverse = invert(gram + jnp.eye(examples, dtype=jnp.float32))
@@ -401,8 +408,8 @@
     classes = at.col * width + jnp.arange(width, dtype=jnp.int32)
     targets = (labels[:, None] == classes[None, :]).astype(jnp.float32)
     gain = matmul(row_side, inverse, BIG)
+    tile = update(inv_corr, gain, col_side, at)
     head = heads + matmul(gain, targets - fitted, BIG)
-    tile = update(inv_corr, gain, col_side, at)
     return (tile, head)
 
 

time: 420 us -> 403 us (0.960)
  waiting for transfers between devices: 102 us -> 151 us
  starting transfers between devices: 84.2 us -> 45.8 us
  Pallas kernels: 155 us -> 145 us
  between operations: 9.63 us -> 1.58 us
  other arithmetic: 30.2 us -> 22.8 us
    ppermute x21, starting transfers between devices: 50.6 us -> 16.8 us  [flip(): return lax.ppermute(value, axis, [(i, i ^ mask) for i in range(size)])]
    ppermute x6, waiting for transfers between devices: 14.9 us -> 37.9 us  [line_step(): lax.ppermute(above, 'col', [(i, i - 1) for i in range(1, at.cols - step +...]
    ppermute x21, waiting for transfers between devices: 84.9 us -> 104 us  [flip(): return lax.ppermute(value, axis, [(i, i ^ mask) for i in range(size)])]
    ppermute x6, starting transfers between devices: 24.5 us -> 15.5 us  [line_step(): lax.ppermute(below, 'col', [(i, i + 1) for i in range(step - 1, at.cols -...]
    pallas_call x1, Pallas kernels: 53.4 us -> 45.5 us  [update(): pl.pallas_call(lambda *refs: update_kernel(len(parts), steps, *refs), gri...]
    ppermute x6, waiting for transfers between devices: 2.48 us -> 9.65 us  [line_step(): lax.ppermute(below, 'col', [(i, i + 1) for i in range(step - 1, at.cols -...]
    pallas_call x4 -> x5, Pallas kernels: 71.7 us -> 69.9 us  [product_step(): pl.pallas_call(lambda *refs: product_kernel(more, last, *refs), grid_spec...]
  transfers between devices with their start and end apart: 34 -> 36, of which waited for: 18 -> 20; matrix products, arithmetic and copies ran while one was open for 11% -> 11% of each run, Pallas kernels for 20% -> 22%
where the time goes in v2:
time: 403 us; the launch traced here: 395 us
  waiting for transfers between devices  151 us (37%)
  Pallas kernels  145 us (36%)
  starting transfers between devices  45.8 us (11%)
  other arithmetic  22.8 us (6%)
  matrix products  16.6 us (4%)
  local copies, waits for them, and re-layouts  12.2 us (3%)
    ppermute x21, waiting for transfers between devices, flip(): return lax.ppermute(value, axis, [(i, i ^ mask) for i in range(size)])  104 us
    pallas_call x5, Pallas kernels, product_step(): pl.pallas_call(lambda *refs: product_kernel(more, last, *refs), grid_spec...  69.9 us
    pallas_call x1, Pallas kernels, update(): pl.pallas_call(lambda *refs: update_kernel(len(parts), steps, *refs), gri...  45.5 us
    ppermute x6, waiting for transfers between devices, line_step(): lax.ppermute(above, 'col', [(i, i - 1) for i in range(1, at.cols - step +...  37.9 us
    pallas_call x4, Pallas kernels, invert(): pl.pallas_call(lambda *refs, which=which: sweep_kernel(which, which == co...  29.9 us
    ppermute x21, starting transfers between devices, flip(): return lax.ppermute(value, axis, [(i, i ^ mask) for i in range(size)])  16.8 us
    dot_general x4, matrix products, product(): lax.dot_general(left, right, (dims, ((), ())), precision=precision, prefe...  16.6 us
    ppermute x6, starting transfers between devices, line_step(): lax.ppermute(below, 'col', [(i, i + 1) for i in range(step - 1, at.cols -...  15.5 us
  transfers between devices with their start and end apart: 36, of which 20 were waited for; matrix products, arithmetic and copies ran while one was open for 11% of the time, Pallas kernels for 22%

profile of v2, /device:TPU:0, one launch (start us, length us, event | category | flops | bytes accessed | tf_op | source)
XLA Modules:
  0.0 395.3 jit_solution(11989526894685581703)
XLA Ops:
  1.9 5.7 %collective-permute-start.1 = (f32[576,512]{1,0:T(8,128)}, f32[576,512]{1,0:T(8,128)S(1)}, u32[]{:S(2)}, u32[]{:S(2)}) collective-permute-start(f32[576,512]{1,0:T(8,128)} %refs_1_.1), channel_id=1, source_target_pairs={{0,1},{1,2},{2,3},{4,5},{5,6},{6,7},{8,9},{9,10},{10,11},{12,13},{... | collective-permute-start | bytes 3538952 | tf_op jit(solution)/shard_map/ppermute | solution.py:73
  8.9 2.7 broadcast.23.clone
  12.8 14.9 %product.3.refs_3_ = f32[512,4608]{1,0:T(8,128)} custom-call(s32[2]{0:T(128)} %pad_add_fusion.2.refs_0_, f32[576,512]{1,0:T(8,128)} %refs_1_.1, f32[2304,4608]{1,0:T(8,128)} %refs_2_.11), custom_call_target="tpu_custom_call" | custom-call | flops 8153726976 | bytes 29491200 | tf_op jit(solution)/shard_map/product/pallas_call | solution.py:282
  27.7 4.1 %collective-permute-done = f32[576,512]{1,0:T(8,128)S(1)} collective-permute-done((f32[576,512]{1,0:T(8,128)}, f32[576,512]{1,0:T(8,128)S(1)}, u32[]{:S(2)}, u32[]{:S(2)}) %collective-permute-start) | collective-permute-done | bytes 1179680 | tf_op jit(solution)/shard_map/ppermute | solution.py:72
  34.3 1.7 collective-permute-start.3
  38.3 16.6 %product.4.refs_3_ = f32[512,4608]{1,0:T(8,128)} custom-call(s32[2]{0:T(128)} %pad_add_fusion.1.refs_0_, f32[576,512]{1,0:T(8,128)} %get-tuple-element.33.refs_1_, f32[2304,4608]{1,0:T(8,128)} %refs_2_.11, f32[512,4608]{1,0:T(8,128)} %product.3.refs_3_), custom_call_target="tpu_custom_call" | custom-call | flops 8153726976 | bytes 29491200 | tf_op jit(solution)/shard_map/product/pallas_call | solution.py:282
  54.9 7.5 %collective-permute-done.2 = f32[576,512]{1,0:T(8,128)S(1)} collective-permute-done((f32[576,512]{1,0:T(8,128)S(1)}, f32[576,512]{1,0:T(8,128)S(1)}, u32[]{:S(2)}, u32[]{:S(2)}) %collective-permute-start.2) | collective-permute-done | bytes 1179680 | tf_op jit(solution)/shard_map/ppermute | solution.py:72
  63.7 1.7 collective-permute-start.5
  66.0 3.0 bitcast_dynamic-update-slice_fusion.5
  69.0 16.6 %product.5.refs_3_ = f32[512,4608]{1,0:T(8,128)} custom-call(s32[2]{0:T(128)} %pad_add_fusion.refs_0_, f32[576,512]{1,0:T(8,128)} %get-tuple-element.31.refs_1_, f32[2304,4608]{1,0:T(8,128)} %refs_2_.11, f32[512,4608]{1,0:T(8,128)} %product.4.refs_3_), custom_call_target="tpu_custom_call" | custom-call | flops 8153726976 | bytes 29491200 | tf_op jit(solution)/shard_map/product/pallas_call | solution.py:282
  85.6 5.0 %collective-permute-done.4 = f32[576,512]{1,0:T(8,128)S(1)} collective-permute-done((f32[576,512]{1,0:T(8,128)S(1)}, f32[576,512]{1,0:T(8,128)S(1)}, u32[]{:S(2)}, u32[]{:S(2)}) %collective-permute-start.4) | collective-permute-done | bytes 1179680 | tf_op jit(solution)/shard_map/ppermute | solution.py:72
  90.7 1.8 bitcast_dynamic-update-slice_fusion.4
  92.5 11.0 %product_last.2 = f32[2304,512]{1,0:T(8,128)} custom-call(s32[2]{0:T(128)} %pad_add_fusion.3.refs_0_, f32[576,512]{1,0:T(8,128)} %get-tuple-element.29.refs_1_, f32[2304,4608]{1,0:T(8,128)} %refs_2_.11, f32[512,4608]{1,0:T(8,128)} %product.5.refs_3_), custom_call_target="tpu_custom_call" | custom-call | flops 4076863488 | bytes 14745600 | tf_op jit(solution)/shard_map/product_last/pallas_call | solution.py:282
  103.4 1.9 collective-permute-start.18
  106.0 10.8 %product_last.3 = f32[2304,512]{1,0:T(8,128)} custom-call(s32[2]{0:T(128)} %pad_add_fusion.4.refs_0_, f32[576,512]{1,0:T(8,128)} %get-tuple-element.29.refs_1_, f32[2304,4608]{1,0:T(8,128)} %refs_2_.11, f32[512,4608]{1,0:T(8,128)} %product.5.refs_3_), custom_call_target="tpu_custom_call" | custom-call | flops 4076863488 | bytes 14745600 | tf_op jit(solution)/shard_map/product_last/pallas_call | solution.py:282
  116.9 4.9 %add.206 = f32[2304,512]{1,0:T(8,128)S(1)} add(f32[2304,512]{1,0:T(8,128)} %collective-permute-done.6, f32[2304,512]{1,0:T(8,128)} %product_last.3) | non-fusion elementwise | flops 1179648 | bytes 14155776 | tf_op jit(solution)/shard_map/add | solution.py:371
  124.1 2.8 collective-permute-start.9
  128.1 1.9 collective-permute-start.19
  130.0 28.6 %collective-permute-done.9 = f32[2,288,512]{2,1,0:T(8,128)} collective-permute-done((f32[2,288,512]{2,1,0:T(8,128)}, f32[2,288,512]{2,1,0:T(8,128)}, u32[]{:S(2)}, u32[]{:S(2)}) %collective-permute-start.9) | collective-permute-done | bytes 1179680 | tf_op jit(solution)/shard_map/ppermute | solution.py:68
  158.6 1.9 bitcast_add_fusion
  160.5 2.5 collective-permute-start.10
  163.1 1.7 bitcast_add_fusion.1
  165.1 6.3 %fusion.8 = f32[512,256]{1,0:T(8,128)S(1)} fusion(f32[2304,512]{1,0:T(8,128)} %bitcast.22, f32[2304,256]{1,0:T(8,128)S(1)} %copy-done.2), kind=kOutput, calls=%fused_computation.64 | convolution fusion | flops 1811939328 | bytes 7602176 | tf_op jit(solution)/shard_map/dot_general | solution.py:17
  171.4 5.2 %collective-permute-done.10 = f32[288,512]{1,0:T(8,128)S(1)} collective-permute-done((f32[288,512]{1,0:T(8,128)S(1)}, f32[288,512]{1,0:T(8,128)S(1)}, u32[]{:S(2)}, u32[]{:S(2)}) %collective-permute-start.10) | collective-permute-done | bytes 589856 | tf_op jit(solution)/shard_map/ppermute | solution.py:68
  176.7 3.2 collective-permute-done.8
  180.1 2.7 fusion.9
  183.0 2.0 collective-permute-done.20
  186.5 1.7 collective-permute-start.11
  188.2 31.6 %collective-permute-done.21 = f32[2,64,512]{2,1,0:T(8,128)S(1)} collective-permute-done((f32[2,64,512]{2,1,0:T(8,128)S(1)}, f32[2,64,512]{2,1,0:T(8,128)S(1)}, u32[]{:S(2)}, u32[]{:S(2)}) %collective-permute-start.21) | collective-permute-done | bytes 262176 | tf_op jit(solution)/shard_map/ppermute | solution.py:68
  220.0 4.9 %collective-permute-done.22 = f32[64,512]{1,0:T(8,128)S(1)} collective-permute-done((f32[64,512]{1,0:T(8,128)S(1)}, f32[64,512]{1,0:T(8,128)S(1)}, u32[]{:S(2)}, u32[]{:S(2)}) %collective-permute-start.22) | collective-permute-done | bytes 131104 | tf_op jit(solution)/shard_map/ppermute | solution.py:68
  225.3 4.7 %collective-permute-done.23 = f32[64,512]{1,0:T(8,128)S(1)} collective-permute-done((f32[64,512]{1,0:T(8,128)S(1)}, f32[64,512]{1,0:T(8,128)S(1)}, u32[]{:S(2)}, u32[]{:S(2)}) %collective-permute-start.23) | collective-permute-done | bytes 131104 | tf_op jit(solution)/shard_map/ppermute | solution.py:68
  230.0 5.9 %collective-permute-start.24 = (f32[64,512]{1,0:T(8,128)S(1)}, f32[64,512]{1,0:T(8,128)S(1)}, u32[]{:S(2)}, u32[]{:S(2)}) collective-permute-start(f32[64,512]{1,0:T(8,128)S(1)} %add.239), channel_id=1, source_target_pairs={{0,2},{1,3},{2,0},{3,1},{4,6},{5,7},{6,4},{7,5},{8,10},{9,11},{10,... | collective-permute-start | bytes 393224 | tf_op jit(solution)/shard_map/ppermute | solution.py:68
  235.9 4.3 %collective-permute-done.24 = f32[64,512]{1,0:T(8,128)S(1)} collective-permute-done((f32[64,512]{1,0:T(8,128)S(1)}, f32[64,512]{1,0:T(8,128)S(1)}, u32[]{:S(2)}, u32[]{:S(2)}) %collective-permute-start.24) | collective-permute-done | bytes 131104 | tf_op jit(solution)/shard_map/ppermute | solution.py:68
  240.8 1.7 collective-permute-start.28
  248.8 7.2 %collective-permute-done.26 = f32[2,64,512]{2,1,0:T(8,128)S(1)} collective-permute-done((f32[2,64,512]{2,1,0:T(8,128)S(1)}, f32[2,64,512]{2,1,0:T(8,128)S(1)}, u32[]{:S(2)}, u32[]{:S(2)}) %collective-permute-start.26) | collective-permute-done | bytes 262176 | tf_op jit(solution)/shard_map/ppermute | solution.py:68
  256.0 5.0 %collective-permute-start.13 = (f32[576,512]{1,0:T(8,128)}, f32[576,512]{1,0:T(8,128)S(1)}, u32[]{:S(2)}, u32[]{:S(2)}) collective-permute-start(f32[576,512]{1,0:T(8,128)} %collective-permute-done.11), channel_id=1, source_target_pairs={{0,1},{1,2},{2,3},{4,5},{5,6},{6,7},{8,9},{9,10},{10,11},{12,13},{... | collective-permute-start | bytes 3538952 | tf_op jit(solution)/shard_map/ppermute | solution.py:73
  263.7 7.5 %sweep_0.1.refs_0_ = f32[512,512]{1,0:T(8,128)S(1)} custom-call(f32[512,512]{1,0:T(8,128)S(1)} %bitcast_add_fusion.2.refs_0_), custom_call_target="tpu_custom_call" | custom-call | flops 10000000000 | bytes 2097152 | tf_op jit(solution)/shard_map/sweep_0/pallas_call | solution.py:227
  271.1 8.3 %collective-permute-done.13 = f32[576,512]{1,0:T(8,128)S(1)} collective-permute-done((f32[576,512]{1,0:T(8,128)}, f32[576,512]{1,0:T(8,128)S(1)}, u32[]{:S(2)}, u32[]{:S(2)}) %collective-permute-start.13) | collective-permute-done | bytes 1179680 | tf_op jit(solution)/shard_map/ppermute | solution.py:73
  281.5 8.5 %collective-permute-done.31 = f32[2,288,512]{2,1,0:T(8,128)S(1)} collective-permute-done((f32[2,288,512]{2,1,0:T(8,128)S(1)}, f32[2,288,512]{2,1,0:T(8,128)S(1)}, u32[]{:S(2)}, u32[]{:S(2)}) %collective-permute-start.31) | collective-permute-done | bytes 1179680 | tf_op jit(solution)/shard_map/ppermute | solution.py:68
  292.9 7.5 %sweep_1.1.refs_0_ = f32[512,512]{1,0:T(8,128)S(1)} custom-call(f32[512,512]{1,0:T(8,128)S(1)} %sweep_0.1.refs_0_), custom_call_target="tpu_custom_call" | custom-call | flops 10000000000 | bytes 2097152 | tf_op jit(solution)/shard_map/sweep_1/pallas_call | solution.py:227
  301.2 7.5 %sweep_2.1.refs_0_ = f32[512,512]{1,0:T(8,128)S(1)} custom-call(f32[512,512]{1,0:T(8,128)S(1)} %sweep_1.1.refs_0_), custom_call_target="tpu_custom_call" | custom-call | flops 10000000000 | bytes 2097152 | tf_op jit(solution)/shard_map/sweep_2/pallas_call | solution.py:227
  308.6 1.8 collective-permute-done.16
  311.9 7.5 %sweep_3.1 = f32[512,512]{1,0:T(8,128)S(1)} custom-call(f32[512,512]{1,0:T(8,128)S(1)} %sweep_2.1.refs_0_), custom_call_target="tpu_custom_call" | custom-call | flops 10000000000 | bytes 2097152 | tf_op jit(solution)/shard_map/sweep_3/pallas_call | solution.py:227
  319.9 19.5 %collective-permute-done.17 = f32[576,512]{1,0:T(8,128)S(1)} collective-permute-done((f32[576,512]{1,0:T(8,128)S(1)}, f32[576,512]{1,0:T(8,128)S(1)}, u32[]{:S(2)}, u32[]{:S(2)}) %collective-permute-start.17) | collective-permute-done | bytes 1179680 | tf_op jit(solution)/shard_map/ppermute | solution.py:72
  339.7 3.9 fusion.10.refs_1_
  343.6 3.7 convolution_add_fusion
  347.3 2.2 copy-done.8
  349.6 45.5 %update.1 = f32[2304,4608]{1,0:T(8,128)} custom-call(s32[1]{0:T(128)} %bitcast.refs_0_, f32[2304,512]{1,0:T(8,128)} %copy-done, f32[2304,4608]{1,0:T(8,128)} %refs_2_.11, f32[2304,512]{1,0:T(8,128)} %bitcast.110, f32[2304,512]{1,0:T(8,128)} %copy-done.8), custom_call_target="tpu_custom_call" | custom-call | flops 32614907904 | bytes 84934656 | tf_op jit(solution)/shard_map/update/pallas_call | solution.py:325
  (109 shorter events, 34.6 us)
Async XLA Ops:
  0.6 31.1 %collective-permute-start = (f32[576,512]{1,0:T(8,128)}, f32[576,512]{1,0:T(8,128)S(1)}, u32[]{:S(2)}, u32[]{:S(2)}) collective-permute-start(f32[576,512]{1,0:T(8,128)} %refs_1_.1), channel_id=1, source_target_pairs={{1,0},{2,1},{3,2},{5,4},{6,5},{7,6},{9,8},{10,9},{11,10},{13,12},{... | collective-permute-start | bytes 3538952 | tf_op jit(solution)/shard_map/ppermute | solution.py:72
  1.9 31.1 %collective-permute-start.1 = (f32[576,512]{1,0:T(8,128)}, f32[576,512]{1,0:T(8,128)S(1)}, u32[]{:S(2)}, u32[]{:S(2)}) collective-permute-start(f32[576,512]{1,0:T(8,128)} %refs_1_.1), channel_id=1, source_target_pairs={{0,1},{1,2},{2,3},{4,5},{5,6},{6,7},{8,9},{9,10},{10,11},{12,13},{... | collective-permute-start | bytes 3538952 | tf_op jit(solution)/shard_map/ppermute | solution.py:73
  8.9 2.7 copy-start.4
  33.0 29.4 %collective-permute-start.2 = (f32[576,512]{1,0:T(8,128)S(1)}, f32[576,512]{1,0:T(8,128)S(1)}, u32[]{:S(2)}, u32[]{:S(2)}) collective-permute-start(f32[576,512]{1,0:T(8,128)S(1)} %collective-permute-done), channel_id=1, source_target_pairs={{1,0},{2,1},{5,4},{6,5},{9,8},{10,9},{13,12},{14,13},{17,16},{18,1... | collective-permute-start | bytes 3538952 | tf_op jit(solution)/shard_map/ppermute | solution.py:72
  34.3 28.1 %collective-permute-start.3 = (f32[576,512]{1,0:T(8,128)S(1)}, f32[576,512]{1,0:T(8,128)}, u32[]{:S(2)}, u32[]{:S(2)}) collective-permute-start(f32[576,512]{1,0:T(8,128)S(1)} %collective-permute-done.1), channel_id=1, source_target_pairs={{1,2},{2,3},{5,6},{6,7},{9,10},{10,11},{13,14},{14,15},{17,18},{18... | collective-permute-start | bytes 3538952 | tf_op jit(solution)/shard_map/ppermute | solution.py:73
  62.4 28.2 %collective-permute-start.4 = (f32[576,512]{1,0:T(8,128)S(1)}, f32[576,512]{1,0:T(8,128)S(1)}, u32[]{:S(2)}, u32[]{:S(2)}) collective-permute-start(f32[576,512]{1,0:T(8,128)S(1)} %collective-permute-done.2), channel_id=1, source_target_pairs={{1,0},{5,4},{9,8},{13,12},{17,16},{21,20},{25,24},{29,28}} | collective-permute-start | bytes 3538952 | tf_op jit(solution)/shard_map/ppermute | solution.py:72
  63.7 26.9 %collective-permute-start.5 = (f32[576,512]{1,0:T(8,128)}, f32[576,512]{1,0:T(8,128)}, u32[]{:S(2)}, u32[]{:S(2)}) collective-permute-start(f32[576,512]{1,0:T(8,128)} %collective-permute-done.3), channel_id=1, source_target_pairs={{2,3},{6,7},{10,11},{14,15},{18,19},{22,23},{26,27},{30,31}} | collective-permute-start | bytes 3538952 | tf_op jit(solution)/shard_map/ppermute | solution.py:73
  92.5 11.0 %copy-start.5 = (f32[576,512]{1,0:T(8,128)S(1)}, f32[576,512]{1,0:T(8,128)}, u32[]{:S(2)}) copy-start(f32[576,512]{1,0:T(8,128)} %refs_1_.1) | copy-start | bytes 3538948
  103.4 13.4 %collective-permute-start.6 = (f32[2304,512]{1,0:T(8,128)}, f32[2304,512]{1,0:T(8,128)}, u32[]{:S(2)}, u32[]{:S(2)}) collective-permute-start(f32[2304,512]{1,0:T(8,128)} %product_last.2), channel_id=1, source_target_pairs={{0,4},{4,0},{8,12},{12,8},{16,20},{20,16},{24,28},{28,24},{1,5},{5... | collective-permute-start | bytes 14155784 | tf_op jit(solution)/shard_map/ppermute | solution.py:68
  103.4 24.7 %collective-permute-start.18 = (f32[576,512]{1,0:T(8,128)S(1)}, f32[576,512]{1,0:T(8,128)}, u32[]{:S(2)}, u32[]{:S(2)}) collective-permute-start(f32[576,512]{1,0:T(8,128)S(1)} %copy-done.5), channel_id=1, source_target_pairs={{0,0},{10,2},{17,1},{27,3},{4,4},{14,6},{21,5},{31,7},{1,9},{11,11... | collective-permute-start | bytes 3538952 | tf_op jit(solution)/shard_map/ppermute | solution.py:138
  122.3 1.8 copy-start.1
  124.1 34.5 %collective-permute-start.9 = (f32[2,288,512]{2,1,0:T(8,128)}, f32[2,288,512]{2,1,0:T(8,128)}, u32[]{:S(2)}, u32[]{:S(2)}) collective-permute-start(f32[2,288,512]{2,1,0:T(8,128)} %dynamic-slice_bitcast_fusion), channel_id=1, source_target_pairs={{0,16},{4,20},{8,24},{12,28},{16,0},{20,4},{24,8},{28,12},{1,17},{... | collective-permute-start | bytes 3538952 | tf_op jit(solution)/shard_map/ppermute | solution.py:68
  128.1 35.0 %collective-permute-start.7 = (f32[2,288,512]{2,1,0:T(8,128)}, f32[2,288,512]{2,1,0:T(8,128)}, u32[]{:S(2)}, u32[]{:S(2)}) collective-permute-start(f32[2,288,512]{2,1,0:T(8,128)} %dynamic-slice_bitcast_fusion.1), channel_id=1, source_target_pairs={{0,8},{4,12},{8,0},{12,4},{16,24},{20,28},{24,16},{28,20},{1,9},{5... | collective-permute-start | bytes 3538952 | tf_op jit(solution)/shard_map/ppermute | solution.py:68
  128.1 52.0 %collective-permute-start.19 = (f32[576,512]{1,0:T(8,128)}, f32[576,512]{1,0:T(8,128)S(1)}, u32[]{:S(2)}, u32[]{:S(2)}) collective-permute-start(f32[576,512]{1,0:T(8,128)} %collective-permute-done.18), channel_id=1, source_target_pairs={{0,0},{2,1},{1,2},{3,3},{4,4},{6,5},{5,6},{7,7},{9,8},{11,9},{8,10... | collective-permute-start | bytes 3538952 | tf_op jit(solution)/shard_map/ppermute | solution.py:139
  160.5 16.1 %collective-permute-start.10 = (f32[288,512]{1,0:T(8,128)S(1)}, f32[288,512]{1,0:T(8,128)S(1)}, u32[]{:S(2)}, u32[]{:S(2)}) collective-permute-start(f32[288,512]{1,0:T(8,128)S(1)} %dynamic-slice_bitcast_fusion.2), channel_id=1, source_target_pairs={{0,8},{4,12},{8,0},{12,4},{16,24},{20,28},{24,16},{28,20},{1,9},{5... | collective-permute-start | bytes 1769480 | tf_op jit(solution)/shard_map/ppermute | solution.py:68
  163.1 2.0 copy-start.2
  164.8 15.1 %collective-permute-start.8 = (f32[288,512]{1,0:T(8,128)S(1)}, f32[288,512]{1,0:T(8,128)S(1)}, u32[]{:S(2)}, u32[]{:S(2)}) collective-permute-start(f32[288,512]{1,0:T(8,128)S(1)} %dynamic-slice_bitcast_fusion.3), channel_id=1, source_target_pairs={{0,16},{4,20},{8,24},{12,28},{16,0},{20,4},{24,8},{28,12},{1,17},{... | collective-permute-start | bytes 1769480 | tf_op jit(solution)/shard_map/ppermute | solution.py:68
  182.9 2.1 collective-permute-start.20
  186.1 33.7 %collective-permute-start.21 = (f32[2,64,512]{2,1,0:T(8,128)S(1)}, f32[2,64,512]{2,1,0:T(8,128)S(1)}, u32[]{:S(2)}, u32[]{:S(2)}) collective-permute-start(f32[2,64,512]{2,1,0:T(8,128)S(1)} %dynamic-slice_bitcast_fusion.5), channel_id=1, source_target_pairs={{0,8},{4,12},{8,0},{12,4},{16,24},{20,28},{24,16},{28,20},{1,9},{5... | collective-permute-start | bytes 786440 | tf_op jit(solution)/shard_map/ppermute | solution.py:68
  186.5 57.6 %collective-permute-start.11 = (f32[576,512]{1,0:T(8,128)S(1)}, f32[576,512]{1,0:T(8,128)}, u32[]{:S(2)}, u32[]{:S(2)}) collective-permute-start(f32[576,512]{1,0:T(8,128)S(1)} %pad_maximum_fusion.3), channel_id=1, source_target_pairs={{0,0},{1,10},{2,17},{3,27},{4,4},{5,14},{6,21},{7,31},{8,1},{9,11}... | collective-permute-start | bytes 3538952 | tf_op jit(solution)/shard_map/ppermute | solution.py:130
  188.2 36.8 %collective-permute-start.33 = (f32[512,256]{1,0:T(8,128)S(1)}, f32[512,256]{1,0:T(8,128)S(1)}, u32[]{:S(2)}, u32[]{:S(2)}) collective-permute-start(f32[512,256]{1,0:T(8,128)S(1)} %fusion.8), channel_id=1, source_target_pairs={{0,4},{4,0},{8,12},{12,8},{16,20},{20,16},{24,28},{28,24},{1,5},{5... | collective-permute-start | bytes 1572872 | tf_op jit(solution)/shard_map/ppermute | solution.py:68
  219.9 5.0 %collective-permute-start.22 = (f32[64,512]{1,0:T(8,128)S(1)}, f32[64,512]{1,0:T(8,128)S(1)}, u32[]{:S(2)}, u32[]{:S(2)}) collective-permute-start(f32[64,512]{1,0:T(8,128)S(1)} %dynamic-slice_bitcast_fusion.6), channel_id=1, source_target_pairs={{0,16},{4,20},{8,24},{12,28},{16,0},{20,4},{24,8},{28,12},{1,17},{... | collective-permute-start | bytes 393224 | tf_op jit(solution)/shard_map/ppermute | solution.py:68
  224.9 5.0 %collective-permute-start.23 = (f32[64,512]{1,0:T(8,128)S(1)}, f32[64,512]{1,0:T(8,128)S(1)}, u32[]{:S(2)}, u32[]{:S(2)}) collective-permute-start(f32[64,512]{1,0:T(8,128)S(1)} %bitcast_add_fusion.7), channel_id=1, source_target_pairs={{0,1},{1,0},{2,3},{3,2},{4,5},{5,4},{6,7},{7,6},{8,9},{9,8},{10,11... | collective-permute-start | bytes 393224 | tf_op jit(solution)/shard_map/ppermute | solution.py:68
  225.1 17.4 %collective-permute-start.34 = (f32[512,256]{1,0:T(8,128)S(1)}, f32[512,256]{1,0:T(8,128)S(1)}, u32[]{:S(2)}, u32[]{:S(2)}) collective-permute-start(f32[512,256]{1,0:T(8,128)S(1)} %add.244), channel_id=1, source_target_pairs={{0,8},{4,12},{8,0},{12,4},{16,24},{20,28},{24,16},{28,20},{1,9},{5... | collective-permute-start | bytes 1572872 | tf_op jit(solution)/shard_map/ppermute | solution.py:68
  230.0 10.3 %collective-permute-start.24 = (f32[64,512]{1,0:T(8,128)S(1)}, f32[64,512]{1,0:T(8,128)S(1)}, u32[]{:S(2)}, u32[]{:S(2)}) collective-permute-start(f32[64,512]{1,0:T(8,128)S(1)} %add.239), channel_id=1, source_target_pairs={{0,2},{1,3},{2,0},{3,1},{4,6},{5,7},{6,4},{7,5},{8,10},{9,11},{10,... | collective-permute-start | bytes 393224 | tf_op jit(solution)/shard_map/ppermute | solution.py:68
  240.3 6.4 %collective-permute-start.25 = (f32[64,512]{1,0:T(8,128)S(1)}, f32[64,512]{1,0:T(8,128)S(1)}, u32[]{:S(2)}, u32[]{:S(2)}) collective-permute-start(f32[64,512]{1,0:T(8,128)S(1)} %add.240), channel_id=1, source_target_pairs={{0,16},{4,20},{8,24},{12,28},{16,0},{20,4},{24,8},{28,12},{1,17},{... | collective-permute-start | bytes 393224 | tf_op jit(solution)/shard_map/ppermute | solution.py:68
  240.8 20.2 %collective-permute-start.28 = (f32[288,512]{1,0:T(8,128)S(1)}, f32[288,512]{1,0:T(8,128)S(1)}, u32[]{:S(2)}, u32[]{:S(2)}) collective-permute-start(f32[288,512]{1,0:T(8,128)S(1)} %get-tuple-element.46), channel_id=1, source_target_pairs={{0,16},{4,20},{8,24},{12,28},{16,0},{20,4},{24,8},{28,12},{1,17},{... | collective-permute-start | bytes 1769480 | tf_op jit(solution)/shard_map/ppermute | solution.py:68
  242.5 18.7 %collective-permute-start.30 = (f32[288,512]{1,0:T(8,128)S(1)}, f32[288,512]{1,0:T(8,128)S(1)}, u32[]{:S(2)}, u32[]{:S(2)}) collective-permute-start(f32[288,512]{1,0:T(8,128)S(1)} %get-tuple-element.47), channel_id=1, source_target_pairs={{0,8},{4,12},{8,0},{12,4},{16,24},{20,28},{24,16},{28,20},{1,9},{5... | collective-permute-start | bytes 1769480 | tf_op jit(solution)/shard_map/ppermute | solution.py:68
  242.6 101.0 %collective-permute-start.35 = (f32[512,256]{1,0:T(8,128)S(1)}, f32[512,256]{1,0:T(8,128)S(1)}, u32[]{:S(2)}, u32[]{:S(2)}) collective-permute-start(f32[512,256]{1,0:T(8,128)S(1)} %add.245), channel_id=1, source_target_pairs={{0,16},{4,20},{8,24},{12,28},{16,0},{20,4},{24,8},{28,12},{1,17},{... | collective-permute-start | bytes 1572872 | tf_op jit(solution)/shard_map/ppermute | solution.py:68
  244.1 36.2 %collective-permute-start.12 = (f32[576,512]{1,0:T(8,128)}, f32[576,512]{1,0:T(8,128)S(1)}, u32[]{:S(2)}, u32[]{:S(2)}) collective-permute-start(f32[576,512]{1,0:T(8,128)} %collective-permute-done.11), channel_id=1, source_target_pairs={{1,0},{2,1},{3,2},{5,4},{6,5},{7,6},{9,8},{10,9},{11,10},{13,12},{... | collective-permute-start | bytes 3538952 | tf_op jit(solution)/shard_map/ppermute | solution.py:72
  246.8 9.2 %collective-permute-start.26 = (f32[2,64,512]{2,1,0:T(8,128)S(1)}, f32[2,64,512]{2,1,0:T(8,128)S(1)}, u32[]{:S(2)}, u32[]{:S(2)}) collective-permute-start(f32[2,64,512]{2,1,0:T(8,128)S(1)} %pad_maximum_fusion.8), channel_id=1, source_target_pairs={{0,8},{4,12},{8,0},{12,4},{16,24},{20,28},{24,16},{28,20},{1,9},{5... | collective-permute-start | bytes 786440 | tf_op jit(solution)/shard_map/ppermute | solution.py:68
  256.0 23.5 %collective-permute-start.13 = (f32[576,512]{1,0:T(8,128)}, f32[576,512]{1,0:T(8,128)S(1)}, u32[]{:S(2)}, u32[]{:S(2)}) collective-permute-start(f32[576,512]{1,0:T(8,128)} %collective-permute-done.11), channel_id=1, source_target_pairs={{0,1},{1,2},{2,3},{4,5},{5,6},{6,7},{8,9},{9,10},{10,11},{12,13},{... | collective-permute-start | bytes 3538952 | tf_op jit(solution)/shard_map/ppermute | solution.py:73
  261.1 2.0 collective-permute-start.27
  261.6 28.4 %collective-permute-start.31 = (f32[2,288,512]{2,1,0:T(8,128)S(1)}, f32[2,288,512]{2,1,0:T(8,128)S(1)}, u32[]{:S(2)}, u32[]{:S(2)}) collective-permute-start(f32[2,288,512]{2,1,0:T(8,128)S(1)} %pad_maximum_fusion.5), channel_id=1, source_target_pairs={{0,16},{4,20},{8,24},{12,28},{16,0},{20,4},{24,8},{28,12},{1,17},{... | collective-permute-start | bytes 3538952 | tf_op jit(solution)/shard_map/ppermute | solution.py:68
  263.1 28.0 %collective-permute-start.29 = (f32[2,288,512]{2,1,0:T(8,128)S(1)}, f32[2,288,512]{2,1,0:T(8,128)S(1)}, u32[]{:S(2)}, u32[]{:S(2)}) collective-permute-start(f32[2,288,512]{2,1,0:T(8,128)S(1)} %pad_maximum_fusion.4), channel_id=1, source_target_pairs={{0,8},{4,12},{8,0},{12,4},{16,24},{20,28},{24,16},{28,20},{1,9},{5... | collective-permute-start | bytes 3538952 | tf_op jit(solution)/shard_map/ppermute | solution.py:68
  279.5 20.9 %collective-permute-start.14 = (f32[576,512]{1,0:T(8,128)S(1)}, f32[576,512]{1,0:T(8,128)S(1)}, u32[]{:S(2)}, u32[]{:S(2)}) collective-permute-start(f32[576,512]{1,0:T(8,128)S(1)} %collective-permute-done.13), channel_id=1, source_target_pairs={{1,2},{2,3},{5,6},{6,7},{9,10},{10,11},{13,14},{14,15},{17,18},{18... | collective-permute-start | bytes 3538952 | tf_op jit(solution)/shard_map/ppermute | solution.py:73
  280.2 30.2 %collective-permute-start.16 = (f32[576,512]{1,0:T(8,128)S(1)}, f32[576,512]{1,0:T(8,128)S(1)}, u32[]{:S(2)}, u32[]{:S(2)}) collective-permute-start(f32[576,512]{1,0:T(8,128)S(1)} %collective-permute-done.12), channel_id=1, source_target_pairs={{1,0},{2,1},{5,4},{6,5},{9,8},{10,9},{13,12},{14,13},{17,16},{18,1... | collective-permute-start | bytes 3538952 | tf_op jit(solution)/shard_map/ppermute | solution.py:72
  292.8 7.6 %copy-start.6 = (f32[4,576,512]{2,1,0:T(8,128)}, f32[4,576,512]{2,1,0:T(8,128)S(1)}, u32[]{:S(2)}) copy-start(f32[4,576,512]{2,1,0:T(8,128)S(1)} %pad_maximum_fusion) | copy-start | bytes 14155780
  292.9 54.5 %collective-permute-start.32 = (f32[2304,512]{1,0:T(8,128)S(1)}, f32[2304,512]{1,0:T(8,128)S(1)}, u32[]{:S(2)}, u32[]{:S(2)}) collective-permute-start(f32[2304,512]{1,0:T(8,128)S(1)} %bitcast.109), channel_id=1, source_target_pairs={{0,4},{4,0},{8,12},{12,8},{16,20},{20,16},{24,28},{28,24},{1,5},{5... | collective-permute-start | bytes 14155784 | tf_op jit(solution)/shard_map/ppermute | solution.py:68
  300.4 19.0 %collective-permute-start.15 = (f32[576,512]{1,0:T(8,128)S(1)}, f32[576,512]{1,0:T(8,128)S(1)}, u32[]{:S(2)}, u32[]{:S(2)}) collective-permute-start(f32[576,512]{1,0:T(8,128)S(1)} %collective-permute-done.14), channel_id=1, source_target_pairs={{2,3},{6,7},{10,11},{14,15},{18,19},{22,23},{26,27},{30,31}} | collective-permute-start | bytes 3538952 | tf_op jit(solution)/shard_map/ppermute | solution.py:73
  310.5 29.0 %collective-permute-start.17 = (f32[576,512]{1,0:T(8,128)S(1)}, f32[576,512]{1,0:T(8,128)S(1)}, u32[]{:S(2)}, u32[]{:S(2)}) collective-permute-start(f32[576,512]{1,0:T(8,128)S(1)} %collective-permute-done.16), channel_id=1, source_target_pairs={{1,0},{5,4},{9,8},{13,12},{17,16},{21,20},{25,24},{29,28}} | collective-permute-start | bytes 3538952 | tf_op jit(solution)/shard_map/ppermute | solution.py:72
  339.7 3.9 copy-start.3
  339.7 3.9 copy-start.7
  343.6 3.7 copy-start
  347.3 2.2 copy-start.8
